TPU v7x, 512 devices: a whole 4x8x8 slice. The times are simulated.
512 devices in a mesh: row: 32 (over y_lo, z), col: 16 (over y_hi, x, core).
Axes of the slice: x: 4, y: 8 (y_hi: 2, y_lo: 4; y = y_hi * 4 + y_lo), z: 8, core: 2. Of those that a mesh axis runs over, the one named last changes fastest.
Arguments:
- amplitudes: bfloat16 [65536, 16384], P(('row', 'col')), may hold values from -6 to 6
- amp_tiles: int32 [1024, 256], P(('row', 'col')), may hold values 0 or 1
- integrals: bfloat16 [512, 16384], P('row', 'col'), may hold values from -0.046875 to 0.046875
- int_tiles: int32 [8, 256], P(None, 'col'), may hold values 0 or 1
Outputs:
- ladder: bfloat16 [512, 65536], P('col', 'row')
All inputs are finite; a program needn't handle non-finite values. No bound on the sum of `amp_tiles` or of `int_tiles` on one device may be relied on, other than what follows from the above.
Results may differ from a plain program's by a relative error of at most 0.001.
Values may be sent and summed in bfloat16 or wider, within the bound.
No kernel may reach another device: no remote copies, remote signals or barrier semaphores. Data moves between devices by JAX's collectives and lax.ppermute only.
A program may use at most 64 MiB of HBM per device.

v0:
```python
import jax
import jax.numpy as jnp
from jax import lax
from jax.experimental import pallas as pl
from jax.experimental.pallas import tpu as pltpu
from jax.sharding import Mesh, PartitionSpec as P

TILE = 64
YLO, Z, YHI, XH, XP, CORE = 4, 8, 2, 2, 2, 2
Y = YHI * YLO
QUADS = YHI * XH
PANEL = 1024
ROWS = 16
PAIRS = 128
TEAM = XP * CORE
ALL = ("ylo", "z", "yhi", "xh", "xp", "core")


def place(y, z, xh, xp, core):
    return ((((y % YLO * Z + z) * YHI + y // YLO) * XH + xh) * XP + xp) * CORE + core


def plane_groups():
    groups = []
    for xp in range(XP):
        groups += [[place(y, z, xh, xp, 0) for xh in range(XH) for y in range(Y)] for z in range(Z)]
        groups += [[place(y, z, xh, xp, 1) for xh in range(XH) for z in range(Z)] for y in range(Y)]
    return groups


def ring_pairs(step):
    pairs = []
    for xh in range(XH):
        for xp in range(XP):
            for y in range(Y):
                for z in range(Z):
                    pairs.append((place(y, z, xh, xp, 0), place(y, (z + step) % Z, xh, xp, 0)))
                    pairs.append((place(y, z, xh, xp, 1), place((y + step) % Y, z, xh, xp, 1)))
    return sorted(pairs)


def spread(tiles):
    tile = lax.broadcasted_iota(jnp.int32, (PANEL // TILE, PANEL), 0)
    lane = lax.broadcasted_iota(jnp.int32, (PANEL // TILE, PANEL), 1)
    picks = (lane // TILE == tile).astype(jnp.bfloat16)
    flags = tiles.astype(jnp.float32).astype(jnp.bfloat16)
    return jnp.dot(flags, picks, preferred_element_type=jnp.float32)


def integral_kernel(meta, ints_hbm, tiles_hbm, out_ref, ints, tiles, sem):
    copies = [
        pltpu.make_async_copy(ints_hbm, ints, sem.at[0]),
        pltpu.make_async_copy(tiles_hbm, tiles, sem.at[1]),
    ]
    for copy in copies:
        copy.start()
    for copy in copies:
        copy.wait()
    wanted = lax.broadcasted_iota(jnp.int32, (8, PANEL // TILE), 0) == meta[2]
    row = jnp.sum(jnp.where(wanted, tiles[...], 0), axis=0, keepdims=True)
    flags = spread(jnp.broadcast_to(row, (8, PANEL // TILE)))[:1]
    masked = (ints[...].astype(jnp.float32) * flags).astype(jnp.bfloat16)
    out_ref[...] = jnp.broadcast_to(masked[None], out_ref.shape)


def split_kernel(meta, *refs):
    own, swap, across = refs[2 * TEAM :]
    outs = (own.at[0], swap.at[0], across.at[0, 0], across.at[1, 0])
    for values, tiles, out in zip(refs[:TEAM], refs[TEAM : 2 * TEAM], outs, strict=True):
        flags = spread(tiles[0])
        for part in range(PAIRS // TILE):
            rows = pl.ds(part * TILE, TILE)
            out[rows, :] = (values[rows, :].astype(jnp.float32) * flags[part : part + 1]).astype(jnp.bfloat16)


def split_amplitudes(meta, amplitudes, amp_tiles):
    tiles = amp_tiles.reshape(PAIRS // TILE, QUADS * TEAM, PANEL // TILE).transpose(1, 0, 2)

    def values(n):
        return pl.BlockSpec((PAIRS, PANEL), lambda i, m: (0, TEAM * i + (m[3] ^ n)))

    def flags(n):
        return pl.BlockSpec((1, PAIRS // TILE, PANEL // TILE), lambda i, m: (TEAM * i + (m[3] ^ n), 0, 0))

    block = pl.BlockSpec((1, PAIRS, PANEL), lambda i, m: (i, 0, 0))
    shape = (QUADS, PAIRS, PANEL)
    return pl.pallas_call(
        split_kernel,
        grid_spec=pltpu.PrefetchScalarGridSpec(
            num_scalar_prefetch=1,
            grid=(QUADS,),
            in_specs=[values(n) for n in range(TEAM)] + [flags(n) for n in range(TEAM)],
            out_specs=[block, block, pl.BlockSpec((CORE, 1, PAIRS, PANEL), lambda i, m: (0, i, 0, 0))],
        ),
        out_shape=[jax.ShapeDtypeStruct(s, jnp.bfloat16) for s in (shape, shape, (CORE,) + shape)],
        compiler_params=pltpu.CompilerParams(vmem_limit_bytes=60 << 20),
        cost_estimate=pl.CostEstimate(flops=8 << 20, bytes_accessed=8 << 20, transcendentals=0),
        name="split_amplitudes",
    )(meta, *[amplitudes] * TEAM, *[tiles] * TEAM)


MEMBERS = XH * 8
SLOTS = [(offset, 0, MEMBERS) for offset in (0, -1, 1, -2, 2, -3, 3)] + [(4, 0, 8), (4, 8, 8)]


def ladder_kernel(meta, *refs):
    blocks, team = refs[: len(SLOTS)], refs[len(SLOTS) : len(SLOTS) + TEAM]
    keep_ref, send_ref, ints, amps, total, sem = refs[len(SLOTS) + TEAM :]
    core, here, me = meta[0], meta[1], meta[3]
    xp = me // CORE

    def copies(on):
        found = []
        for source, (offset, first, members) in zip(blocks, SLOTS, strict=True):
            there = lax.rem(here + offset + 8, 8)
            for xh in range(first // 8, (first + members) // 8):
                at = xh * 8 - first
                if on == 0:
                    for yhi in range(YHI):
                        found.append((source.at[pl.ds(at + yhi * YLO, YLO)], ints.at[yhi * XH + xh, :, there]))
                else:
                    found.append((source.at[pl.ds(at, Z)], ints.at[(there // YLO) * XH + xh, lax.rem(there, YLO)]))
        return [pltpu.make_async_copy(a, b, sem.at[0]) for a, b in found]

    mine = []
    for n in range(TEAM):
        rows = pl.ds(pl.multiple_of((me ^ n) * PAIRS, PAIRS), PAIRS)
        source = team[n].at[0] if n == 2 else team[n]
        mine.append(pltpu.make_async_copy(source, amps.at[:, rows], sem.at[0]))
    for copy in mine:
        copy.start()
    for on in range(CORE):

        @pl.when(core == on)
        def _():
            todo = copies(on)
            for copy in todo:
                copy.start()
            for copy in todo:
                copy.wait()

    for copy in mine:
        copy.wait()
    for panel in range(QUADS):
        product = lax.dot_general(
            ints[panel].reshape(YLO * Z * ROWS, PANEL),
            amps[panel],
            (((1,), (1,)), ((), ())),
            preferred_element_type=jnp.float32,
        ).reshape(total.shape)
        if panel == 0:
            total[...] = product
        else:
            total[...] += product
    for n in range(XP):
        keep_ref[n] = total[:, (xp ^ n) * CORE + core]
        send_ref[n] = total[:, (xp ^ n) * CORE + 1 - core]


def compute(amplitudes, amp_tiles, integrals, int_tiles):
    core = lax.axis_index("core")
    z = lax.axis_index("z")
    ylo = lax.axis_index("ylo")
    y = lax.axis_index("yhi") * YLO + ylo
    me = lax.axis_index("xp") * CORE + core
    meta = jnp.stack([core, jnp.where(core == 0, z, y), (ylo * Z + z) // 4, me]).astype(jnp.int32)

    panels = pl.pallas_call(
        integral_kernel,
        in_specs=[pl.BlockSpec(memory_space=pltpu.SMEM)] + [pl.BlockSpec(memory_space=pltpu.HBM)] * 2,
        out_specs=pl.BlockSpec(memory_space=pltpu.VMEM),
        out_shape=jax.ShapeDtypeStruct((MEMBERS, ROWS, PANEL), jnp.bfloat16),
        scratch_shapes=[
            pltpu.VMEM((ROWS, PANEL), jnp.bfloat16),
            pltpu.VMEM((8, PANEL // TILE), jnp.int32),
            pltpu.SemaphoreType.DMA((2,)),
        ],
        compiler_params=pltpu.CompilerParams(vmem_limit_bytes=60 << 20),
        name="mask_integrals",
    )(meta, integrals, int_tiles)
    plane = lax.all_to_all(panels, ALL, 0, 0, axis_index_groups=plane_groups(), tiled=True)

    own, swap, across = split_amplitudes(meta, amplitudes, amp_tiles)
    across = lax.ppermute(across, "xp", [(0, 1), (1, 0)])
    swap = lax.ppermute(swap, "core", [(0, 1), (1, 0)])
    relay = lax.ppermute(across[1], "core", [(0, 1), (1, 0)])

    up, down = ring_pairs(1), ring_pairs(-1)
    have = {0: plane}
    for step in (1, 2, 3):
        have[-step] = lax.ppermute(have[1 - step], ALL, up)
        have[step] = lax.ppermute(have[step - 1], ALL, down)
    last_up = lax.ppermute(have[-3][:8], ALL, up)
    last_down = lax.ppermute(have[3][8:], ALL, down)
    blocks = [have[offset] for offset, _, _ in SLOTS[:7]] + [last_up, last_down]

    share = jax.ShapeDtypeStruct((XP, QUADS, 32, TEAM * PAIRS), jnp.float32)
    keep, send = pl.pallas_call(
        ladder_kernel,
        in_specs=[pl.BlockSpec(memory_space=pltpu.SMEM)]
        + [pl.BlockSpec(memory_space=pl.ANY)] * (len(SLOTS) + TEAM),
        out_specs=[pl.BlockSpec(memory_space=pltpu.VMEM)] * 2,
        out_shape=(share, share),
        scratch_shapes=[
            pltpu.VMEM((QUADS, YLO, Z, ROWS, PANEL), jnp.bfloat16),
            pltpu.VMEM((QUADS, TEAM * PAIRS, PANEL), jnp.bfloat16),
            pltpu.VMEM((QUADS, TEAM, 32, TEAM * PAIRS), jnp.float32),
            pltpu.SemaphoreType.DMA((1,)),
        ],
        compiler_params=pltpu.CompilerParams(vmem_limit_bytes=24 << 20),
        cost_estimate=pl.CostEstimate(flops=2 << 30, bytes_accessed=10 << 20, transcendentals=0),
        name="ladder",
    )(meta, *blocks, own, swap, across, relay)
    pair = keep + lax.ppermute(send, "core", [(0, 1), (1, 0)])
    summed = (pair[0] + lax.ppermute(pair[1], "xp", [(0, 1), (1, 0)])).astype(jnp.bfloat16)
    pieces = lax.all_to_all(summed, ("yhi", "xh"), 0, 0, tiled=True)
    return pieces.transpose(1, 0, 2).reshape(32, QUADS * TEAM * PAIRS)


def solution(mesh):
    grid = Mesh(mesh.devices.reshape(YLO, Z, YHI, XH, XP, CORE), ALL)
    rows, cols = ("ylo", "z"), ("yhi", "xh", "xp", "core")
    return jax.shard_map(
        compute,
        mesh=grid,
        in_specs=(P(ALL, None), P(ALL, None), P(rows, cols), P(None, cols)),
        out_specs=P(cols, rows),
        check_vma=False,
    )
```

profile of v0, /device:TPU:8, one launch (start us, length us, event | category | flops | bytes accessed | tf_op | source)
XLA Modules:
  0.0 155.5 jit_solution(7807214440174954065)
XLA Ops:
  0.0 0.8 reshape.6
  0.8 0.6 copy.9
  1.4 0.6 pad_add_fusion.meta
  2.0 5.7 %split_amplitudes.1 = (bf16[4,128,1024]{2,1,0:T(8,128)(2,1)}, bf16[4,128,1024]{2,1,0:T(8,128)(2,1)}, bf16[2,4,128,1024]{3,2,1,0:T(8,128)(2,1)}) custom-call(s32[4]{0:T(128)} %pad_add_fusion.meta, bf16[128,16384]{1,0:T(8,128)(2,1)} %refs_3_.1, bf16[128,16384]{1,0:T(8,128)(2,1)} %refs_3_.1, bf16[128,16384]{1,0:T(8,128)(2,1)} %refs_3_.1, ...), custom_call_target="tpu_custom_call" | custom-call | flops 8388608 | bytes 8388608 | tf_op jit(solution)/shard_map/split_amplitudes/pallas_call | solution.py:87
  7.7 3.4 %collective-permute-start.9 = (bf16[2,4,128,1024]{3,2,1,0:T(8,128)(2,1)}, bf16[2,4,128,1024]{3,2,1,0:T(8,128)(2,1)S(1)}, u32[]{:S(2)}, u32[]{:S(2)}) collective-permute-start(bf16[2,4,128,1024]{3,2,1,0:T(8,128)(2,1)} %get-tuple-element.12), channel_id=1, source_target_pairs={{0,2},{2,0},{1,3},{3,1},{4,6},{6,4},{5,7},{7,5},{8,10},{10,8},{9,1... | collective-permute-start | bytes 6291464 | tf_op jit(solution)/shard_map/ppermute | solution.py:184
  11.1 2.4 %mask_integrals.1 = bf16[16,16,1024]{2,1,0:T(8,128)(2,1)} custom-call(s32[4]{0:T(128)} %pad_add_fusion.meta, bf16[16,1024]{1,0:T(8,128)(2,1)} %ints_hbm.1, s32[8,16]{1,0:T(8,128)} %tiles_hbm.1), custom_call_target="tpu_custom_call" | custom-call | tf_op jit(solution)/shard_map/mask_integrals/pallas_call | solution.py:168
  13.6 0.0 copy-start
  13.6 0.0 copy-start.1
  13.6 51.4 %all_to_all.10.refs_0_ = bf16[16,16,1024]{2,1,0:T(8,128)(2,1)S(1)} all-to-all(bf16[16,16,1024]{2,1,0:T(8,128)(2,1)} %mask_integrals.1), channel_id=1, replica_groups={{0,128,256,384,8,136,264,392,4,132,260,388,12,140,268,396},{16,144,272,..., dimensions={0} | all-to-all | bytes 1048576 | tf_op jit(solution)/shard_map/all_to_all | solution.py:181
  65.0 4.3 %collective-permute-start = (bf16[16,16,1024]{2,1,0:T(8,128)(2,1)S(1)}, bf16[16,16,1024]{2,1,0:T(8,128)(2,1)S(1)}, u32[]{:S(2)}, u32[]{:S(2)}) collective-permute-start(bf16[16,16,1024]{2,1,0:T(8,128)(2,1)S(1)} %all_to_all.10.refs_0_), channel_id=1, source_target_pairs={{0,16},{1,129},{2,18},{3,131},{4,20},{5,133},{6,22},{7,135},{8,24}... | collective-permute-start | bytes 1572872 | tf_op jit(solution)/shard_map/ppermute | solution.py:191
  69.3 8.6 %collective-permute-start.1 = (bf16[16,16,1024]{2,1,0:T(8,128)(2,1)S(1)}, bf16[16,16,1024]{2,1,0:T(8,128)(2,1)S(1)}, u32[]{:S(2)}, u32[]{:S(2)}) collective-permute-start(bf16[16,16,1024]{2,1,0:T(8,128)(2,1)S(1)} %all_to_all.10.refs_0_), channel_id=1, source_target_pairs={{0,112},{1,393},{2,114},{3,395},{4,116},{5,397},{6,118},{7,399},{8... | collective-permute-start | bytes 1572872 | tf_op jit(solution)/shard_map/ppermute | solution.py:192
  77.9 1.9 %collective-permute-start.8 = (bf16[4,128,1024]{2,1,0:T(8,128)(2,1)}, bf16[4,128,1024]{2,1,0:T(8,128)(2,1)S(1)}, u32[]{:S(2)}, u32[]{:S(2)}) collective-permute-start(bf16[4,128,1024]{2,1,0:T(8,128)(2,1)} %get-tuple-element.11), channel_id=1, source_target_pairs={{0,1},{1,0},{2,3},{3,2},{4,5},{5,4},{6,7},{7,6},{8,9},{9,8},{10,11... | collective-permute-start | bytes 3145736 | tf_op jit(solution)/shard_map/ppermute | solution.py:185
  79.8 3.3 %collective-permute-done.refs_1_ = bf16[16,16,1024]{2,1,0:T(8,128)(2,1)S(1)} collective-permute-done((bf16[16,16,1024]{2,1,0:T(8,128)(2,1)S(1)}, bf16[16,16,1024]{2,1,0:T(8,128)(2,1)S(1)}, u32[]{:S(2)}, u32[]{:S(2)}) %collective-permute-start) | collective-permute-done | bytes 524320 | tf_op jit(solution)/shard_map/ppermute | solution.py:191
  83.1 1.9 %collective-permute-start.2 = (bf16[16,16,1024]{2,1,0:T(8,128)(2,1)S(1)}, bf16[16,16,1024]{2,1,0:T(8,128)(2,1)S(1)}, u32[]{:S(2)}, u32[]{:S(2)}) collective-permute-start(bf16[16,16,1024]{2,1,0:T(8,128)(2,1)S(1)} %collective-permute-done.refs_1_), channel_id=1, source_target_pairs={{0,16},{1,129},{2,18},{3,131},{4,20},{5,133},{6,22},{7,135},{8,24}... | collective-permute-start | bytes 1572872 | tf_op jit(solution)/shard_map/ppermute | solution.py:191
  85.0 0.0 collective-permute-done.1.refs_2_
  85.0 5.1 %collective-permute-start.3 = (bf16[16,16,1024]{2,1,0:T(8,128)(2,1)S(1)}, bf16[16,16,1024]{2,1,0:T(8,128)(2,1)S(1)}, u32[]{:S(2)}, u32[]{:S(2)}) collective-permute-start(bf16[16,16,1024]{2,1,0:T(8,128)(2,1)S(1)} %collective-permute-done.1.refs_2_), channel_id=1, source_target_pairs={{0,112},{1,393},{2,114},{3,395},{4,116},{5,397},{6,118},{7,399},{8... | collective-permute-start | bytes 1572872 | tf_op jit(solution)/shard_map/ppermute | solution.py:192
  90.2 0.0 collective-permute-done.9.refs_11_
  90.2 0.1 slice_bitcast_fusion
  90.3 1.9 %collective-permute-start.10 = (bf16[4,128,1024]{2,1,0:T(8,128)(2,1)S(1)}, bf16[4,128,1024]{2,1,0:T(8,128)(2,1)S(1)}, u32[]{:S(2)}, u32[]{:S(2)}) collective-permute-start(bf16[4,128,1024]{2,1,0:T(8,128)(2,1)S(1)} %slice_bitcast_fusion), channel_id=1, source_target_pairs={{0,1},{1,0},{2,3},{3,2},{4,5},{5,4},{6,7},{7,6},{8,9},{9,8},{10,11... | collective-permute-start | bytes 3145736 | tf_op jit(solution)/shard_map/ppermute | solution.py:186
  92.2 3.2 %collective-permute-done.2.refs_3_ = bf16[16,16,1024]{2,1,0:T(8,128)(2,1)S(1)} collective-permute-done((bf16[16,16,1024]{2,1,0:T(8,128)(2,1)S(1)}, bf16[16,16,1024]{2,1,0:T(8,128)(2,1)S(1)}, u32[]{:S(2)}, u32[]{:S(2)}) %collective-permute-start.2) | collective-permute-done | bytes 524320 | tf_op jit(solution)/shard_map/ppermute | solution.py:191
  95.4 1.9 %collective-permute-start.4 = (bf16[16,16,1024]{2,1,0:T(8,128)(2,1)S(1)}, bf16[16,16,1024]{2,1,0:T(8,128)(2,1)S(1)}, u32[]{:S(2)}, u32[]{:S(2)}) collective-permute-start(bf16[16,16,1024]{2,1,0:T(8,128)(2,1)S(1)} %collective-permute-done.2.refs_3_), channel_id=1, source_target_pairs={{0,16},{1,129},{2,18},{3,131},{4,20},{5,133},{6,22},{7,135},{8,24}... | collective-permute-start | bytes 1572872 | tf_op jit(solution)/shard_map/ppermute | solution.py:191
  97.3 0.0 collective-permute-done.3.refs_4_
  97.3 5.1 %collective-permute-start.5 = (bf16[16,16,1024]{2,1,0:T(8,128)(2,1)S(1)}, bf16[16,16,1024]{2,1,0:T(8,128)(2,1)S(1)}, u32[]{:S(2)}, u32[]{:S(2)}) collective-permute-start(bf16[16,16,1024]{2,1,0:T(8,128)(2,1)S(1)} %collective-permute-done.3.refs_4_), channel_id=1, source_target_pairs={{0,112},{1,393},{2,114},{3,395},{4,116},{5,397},{6,118},{7,399},{8... | collective-permute-start | bytes 1572872 | tf_op jit(solution)/shard_map/ppermute | solution.py:192
  102.4 5.2 %collective-permute-done.4.refs_5_ = bf16[16,16,1024]{2,1,0:T(8,128)(2,1)S(1)} collective-permute-done((bf16[16,16,1024]{2,1,0:T(8,128)(2,1)S(1)}, bf16[16,16,1024]{2,1,0:T(8,128)(2,1)S(1)}, u32[]{:S(2)}, u32[]{:S(2)}) %collective-permute-start.4) | collective-permute-done | bytes 524320 | tf_op jit(solution)/shard_map/ppermute | solution.py:191
  107.7 1.9 %collective-permute-start.6 = (bf16[8,16,1024]{2,1,0:T(8,128)(2,1)S(1)}, bf16[8,16,1024]{2,1,0:T(8,128)(2,1)S(1)}, u32[]{:S(2)}, u32[]{:S(2)}) collective-permute-start(bf16[8,16,1024]{2,1,0:T(8,128)(2,1)S(1)} %slice.20), channel_id=1, source_target_pairs={{0,16},{1,129},{2,18},{3,131},{4,20},{5,133},{6,22},{7,135},{8,24}... | collective-permute-start | bytes 786440 | tf_op jit(solution)/shard_map/ppermute | solution.py:193
  109.6 0.0 collective-permute-done.5.refs_6_
  109.6 5.1 %collective-permute-start.7 = (bf16[8,16,1024]{2,1,0:T(8,128)(2,1)S(1)}, bf16[8,16,1024]{2,1,0:T(8,128)(2,1)S(1)}, u32[]{:S(2)}, u32[]{:S(2)}) collective-permute-start(bf16[8,16,1024]{2,1,0:T(8,128)(2,1)S(1)} %slice.21), channel_id=1, source_target_pairs={{0,112},{1,393},{2,114},{3,395},{4,116},{5,397},{6,118},{7,399},{8... | collective-permute-start | bytes 786440 | tf_op jit(solution)/shard_map/ppermute | solution.py:194
  114.8 0.0 collective-permute-done.8.refs_10_
  114.8 2.4 %collective-permute-done.6.refs_7_ = bf16[8,16,1024]{2,1,0:T(8,128)(2,1)S(1)} collective-permute-done((bf16[8,16,1024]{2,1,0:T(8,128)(2,1)S(1)}, bf16[8,16,1024]{2,1,0:T(8,128)(2,1)S(1)}, u32[]{:S(2)}, u32[]{:S(2)}) %collective-permute-start.6) | collective-permute-done | bytes 262176 | tf_op jit(solution)/shard_map/ppermute | solution.py:193
  117.1 1.5 collective-permute-done.7.refs_8_
  118.6 0.0 collective-permute-done.10.refs_12_
  118.6 0.0 copy-done
  118.6 0.0 copy-done.1
  118.7 4.7 %ladder.1 = (f32[2,4,32,512]{3,2,1,0:T(8,128)S(1)}, f32[2,4,32,512]{3,2,1,0:T(8,128)S(1)}) custom-call(s32[4]{0:T(128)S(1)} %copy-done.1, bf16[16,16,1024]{2,1,0:T(8,128)(2,1)S(1)} %all_to_all.10.refs_0_, bf16[16,16,1024]{2,1,0:T(8,128)(2,1)S(1)} %collective-permute-done.refs_1_, bf16[16,16,1024]{2,1,0:T(8,128)(2,1)S(1)} %collective-permute-done.1.refs_2_, ...), custom_call_target="tpu_custom_call" | custom-call | flops 2147483648 | bytes 10485760 | tf_op jit(solution)/shard_map/ladder/pallas_call | solution.py:198
  123.3 1.9 %collective-permute-start.11 = (f32[2,4,32,512]{3,2,1,0:T(8,128)S(1)}, f32[2,4,32,512]{3,2,1,0:T(8,128)S(1)}, u32[]{:S(2)}, u32[]{:S(2)}) collective-permute-start(f32[2,4,32,512]{3,2,1,0:T(8,128)S(1)} %get-tuple-element.14), channel_id=1, source_target_pairs={{0,1},{1,0},{2,3},{3,2},{4,5},{5,4},{6,7},{7,6},{8,9},{9,8},{10,11... | collective-permute-start | bytes 1572872 | tf_op jit(solution)/shard_map/ppermute | solution.py:214
  125.2 1.9 %collective-permute-done.11 = f32[2,4,32,512]{3,2,1,0:T(8,128)S(1)} collective-permute-done((f32[2,4,32,512]{3,2,1,0:T(8,128)S(1)}, f32[2,4,32,512]{3,2,1,0:T(8,128)S(1)}, u32[]{:S(2)}, u32[]{:S(2)}) %collective-permute-start.11) | collective-permute-done | bytes 524320 | tf_op jit(solution)/shard_map/ppermute | solution.py:214
  127.1 0.1 add.19
  127.2 2.1 %collective-permute-start.12 = (f32[4,32,512]{2,1,0:T(8,128)S(1)}, f32[4,32,512]{2,1,0:T(8,128)S(1)}, u32[]{:S(2)}, u32[]{:S(2)}) collective-permute-start(f32[4,32,512]{2,1,0:T(8,128)S(1)} %slice_bitcast_fusion.1), channel_id=1, source_target_pairs={{0,2},{2,0},{1,3},{3,1},{4,6},{6,4},{5,7},{7,5},{8,10},{10,8},{9,1... | collective-permute-start | bytes 786440 | tf_op jit(solution)/shard_map/ppermute | solution.py:215
  129.4 8.1 %collective-permute-done.12 = f32[4,32,512]{2,1,0:T(8,128)S(1)} collective-permute-done((f32[4,32,512]{2,1,0:T(8,128)S(1)}, f32[4,32,512]{2,1,0:T(8,128)S(1)}, u32[]{:S(2)}, u32[]{:S(2)}) %collective-permute-start.12) | collective-permute-done | bytes 262176 | tf_op jit(solution)/shard_map/ppermute | solution.py:215
  137.5 17.4 %all_to_all.11 = bf16[4,32,512]{2,1,0:T(8,128)(2,1)S(1)} all-to-all(bf16[4,32,512]{2,1,0:T(8,128)(2,1)S(1)} %fusion.1), channel_id=1, replica_groups=mesh['ylo'=4,'z'=8,'yhi'=2,'xh'=2,'xp'=2,'core'=2] {'yhi','xh'}, dimensions={0} | all-to-all | bytes 262144 | tf_op jit(solution)/shard_map/all_to_all | solution.py:216
  154.9 0.7 copy.7
  (4 shorter events, 0.1 us)
Async XLA Ops:
  7.7 82.4 %collective-permute-start.9 = (bf16[2,4,128,1024]{3,2,1,0:T(8,128)(2,1)}, bf16[2,4,128,1024]{3,2,1,0:T(8,128)(2,1)S(1)}, u32[]{:S(2)}, u32[]{:S(2)}) collective-permute-start(bf16[2,4,128,1024]{3,2,1,0:T(8,128)(2,1)} %get-tuple-element.12), channel_id=1, source_target_pairs={{0,2},{2,0},{1,3},{3,1},{4,6},{6,4},{5,7},{7,5},{8,10},{10,8},{9,1... | collective-permute-start | bytes 6291464 | tf_op jit(solution)/shard_map/ppermute | solution.py:184
  13.6 105.1 %copy-start = (bf16[4,128,1024]{2,1,0:T(8,128)(2,1)S(1)}, bf16[4,128,1024]{2,1,0:T(8,128)(2,1)}, u32[]{:S(2)}) copy-start(bf16[4,128,1024]{2,1,0:T(8,128)(2,1)} %get-tuple-element.10.refs_9_) | copy-start | bytes 3145732
  13.6 105.1 %copy-start.1 = (s32[4]{0:T(128)S(1)}, s32[4]{0:T(128)}, u32[]{:S(2)}) copy-start(s32[4]{0:T(128)} %pad_add_fusion.meta) | copy-start | bytes 52
  65.0 18.1 %collective-permute-start = (bf16[16,16,1024]{2,1,0:T(8,128)(2,1)S(1)}, bf16[16,16,1024]{2,1,0:T(8,128)(2,1)S(1)}, u32[]{:S(2)}, u32[]{:S(2)}) collective-permute-start(bf16[16,16,1024]{2,1,0:T(8,128)(2,1)S(1)} %all_to_all.10.refs_0_), channel_id=1, source_target_pairs={{0,16},{1,129},{2,18},{3,131},{4,20},{5,133},{6,22},{7,135},{8,24}... | collective-permute-start | bytes 1572872 | tf_op jit(solution)/shard_map/ppermute | solution.py:191
  69.3 15.7 %collective-permute-start.1 = (bf16[16,16,1024]{2,1,0:T(8,128)(2,1)S(1)}, bf16[16,16,1024]{2,1,0:T(8,128)(2,1)S(1)}, u32[]{:S(2)}, u32[]{:S(2)}) collective-permute-start(bf16[16,16,1024]{2,1,0:T(8,128)(2,1)S(1)} %all_to_all.10.refs_0_), channel_id=1, source_target_pairs={{0,112},{1,393},{2,114},{3,395},{4,116},{5,397},{6,118},{7,399},{8... | collective-permute-start | bytes 1572872 | tf_op jit(solution)/shard_map/ppermute | solution.py:192
  77.9 36.9 %collective-permute-start.8 = (bf16[4,128,1024]{2,1,0:T(8,128)(2,1)}, bf16[4,128,1024]{2,1,0:T(8,128)(2,1)S(1)}, u32[]{:S(2)}, u32[]{:S(2)}) collective-permute-start(bf16[4,128,1024]{2,1,0:T(8,128)(2,1)} %get-tuple-element.11), channel_id=1, source_target_pairs={{0,1},{1,0},{2,3},{3,2},{4,5},{5,4},{6,7},{7,6},{8,9},{9,8},{10,11... | collective-permute-start | bytes 3145736 | tf_op jit(solution)/shard_map/ppermute | solution.py:185
  83.1 12.3 %collective-permute-start.2 = (bf16[16,16,1024]{2,1,0:T(8,128)(2,1)S(1)}, bf16[16,16,1024]{2,1,0:T(8,128)(2,1)S(1)}, u32[]{:S(2)}, u32[]{:S(2)}) collective-permute-start(bf16[16,16,1024]{2,1,0:T(8,128)(2,1)S(1)} %collective-permute-done.refs_1_), channel_id=1, source_target_pairs={{0,16},{1,129},{2,18},{3,131},{4,20},{5,133},{6,22},{7,135},{8,24}... | collective-permute-start | bytes 1572872 | tf_op jit(solution)/shard_map/ppermute | solution.py:191
  85.0 12.3 %collective-permute-start.3 = (bf16[16,16,1024]{2,1,0:T(8,128)(2,1)S(1)}, bf16[16,16,1024]{2,1,0:T(8,128)(2,1)S(1)}, u32[]{:S(2)}, u32[]{:S(2)}) collective-permute-start(bf16[16,16,1024]{2,1,0:T(8,128)(2,1)S(1)} %collective-permute-done.1.refs_2_), channel_id=1, source_target_pairs={{0,112},{1,393},{2,114},{3,395},{4,116},{5,397},{6,118},{7,399},{8... | collective-permute-start | bytes 1572872 | tf_op jit(solution)/shard_map/ppermute | solution.py:192
  90.3 28.4 %collective-permute-start.10 = (bf16[4,128,1024]{2,1,0:T(8,128)(2,1)S(1)}, bf16[4,128,1024]{2,1,0:T(8,128)(2,1)S(1)}, u32[]{:S(2)}, u32[]{:S(2)}) collective-permute-start(bf16[4,128,1024]{2,1,0:T(8,128)(2,1)S(1)} %slice_bitcast_fusion), channel_id=1, source_target_pairs={{0,1},{1,0},{2,3},{3,2},{4,5},{5,4},{6,7},{7,6},{8,9},{9,8},{10,11... | collective-permute-start | bytes 3145736 | tf_op jit(solution)/shard_map/ppermute | solution.py:186
  95.4 12.3 %collective-permute-start.4 = (bf16[16,16,1024]{2,1,0:T(8,128)(2,1)S(1)}, bf16[16,16,1024]{2,1,0:T(8,128)(2,1)S(1)}, u32[]{:S(2)}, u32[]{:S(2)}) collective-permute-start(bf16[16,16,1024]{2,1,0:T(8,128)(2,1)S(1)} %collective-permute-done.2.refs_3_), channel_id=1, source_target_pairs={{0,16},{1,129},{2,18},{3,131},{4,20},{5,133},{6,22},{7,135},{8,24}... | collective-permute-start | bytes 1572872 | tf_op jit(solution)/shard_map/ppermute | solution.py:191
  97.3 12.3 %collective-permute-start.5 = (bf16[16,16,1024]{2,1,0:T(8,128)(2,1)S(1)}, bf16[16,16,1024]{2,1,0:T(8,128)(2,1)S(1)}, u32[]{:S(2)}, u32[]{:S(2)}) collective-permute-start(bf16[16,16,1024]{2,1,0:T(8,128)(2,1)S(1)} %collective-permute-done.3.refs_4_), channel_id=1, source_target_pairs={{0,112},{1,393},{2,114},{3,395},{4,116},{5,397},{6,118},{7,399},{8... | collective-permute-start | bytes 1572872 | tf_op jit(solution)/shard_map/ppermute | solution.py:192
  107.7 9.5 %collective-permute-start.6 = (bf16[8,16,1024]{2,1,0:T(8,128)(2,1)S(1)}, bf16[8,16,1024]{2,1,0:T(8,128)(2,1)S(1)}, u32[]{:S(2)}, u32[]{:S(2)}) collective-permute-start(bf16[8,16,1024]{2,1,0:T(8,128)(2,1)S(1)} %slice.20), channel_id=1, source_target_pairs={{0,16},{1,129},{2,18},{3,131},{4,20},{5,133},{6,22},{7,135},{8,24}... | collective-permute-start | bytes 786440 | tf_op jit(solution)/shard_map/ppermute | solution.py:193
  109.6 9.0 %collective-permute-start.7 = (bf16[8,16,1024]{2,1,0:T(8,128)(2,1)S(1)}, bf16[8,16,1024]{2,1,0:T(8,128)(2,1)S(1)}, u32[]{:S(2)}, u32[]{:S(2)}) collective-permute-start(bf16[8,16,1024]{2,1,0:T(8,128)(2,1)S(1)} %slice.21), channel_id=1, source_target_pairs={{0,112},{1,393},{2,114},{3,395},{4,116},{5,397},{6,118},{7,399},{8... | collective-permute-start | bytes 786440 | tf_op jit(solution)/shard_map/ppermute | solution.py:194
  123.3 3.8 %collective-permute-start.11 = (f32[2,4,32,512]{3,2,1,0:T(8,128)S(1)}, f32[2,4,32,512]{3,2,1,0:T(8,128)S(1)}, u32[]{:S(2)}, u32[]{:S(2)}) collective-permute-start(f32[2,4,32,512]{3,2,1,0:T(8,128)S(1)} %get-tuple-element.14), channel_id=1, source_target_pairs={{0,1},{1,0},{2,3},{3,2},{4,5},{5,4},{6,7},{7,6},{8,9},{9,8},{10,11... | collective-permute-start | bytes 1572872 | tf_op jit(solution)/shard_map/ppermute | solution.py:214
  127.2 10.2 %collective-permute-start.12 = (f32[4,32,512]{2,1,0:T(8,128)S(1)}, f32[4,32,512]{2,1,0:T(8,128)S(1)}, u32[]{:S(2)}, u32[]{:S(2)}) collective-permute-start(f32[4,32,512]{2,1,0:T(8,128)S(1)} %slice_bitcast_fusion.1), channel_id=1, source_target_pairs={{0,2},{2,0},{1,3},{3,1},{4,6},{6,4},{5,7},{7,5},{8,10},{10,8},{9,1... | collective-permute-start | bytes 786440 | tf_op jit(solution)/shard_map/ppermute | solution.py:215
where the time goes:
time: 156 us
  blocking collectives  68.8 us (44%)
  starting transfers between devices  45.3 us (29%)
  waiting for transfers between devices  25.5 us (16%)
  Pallas kernels  12.8 us (8%)
  local copies, waits for them, and re-layouts  2.17 us (1%)
    all_to_all x1, blocking collectives, compute(): lax.all_to_all(panels, ALL, 0, 0, axis_index_groups=plane_groups(), tiled...  51.4 us
    ppermute x3, starting transfers between devices, compute(): have[step] = lax.ppermute(have[step - 1], ALL, down)  18.9 us
    all_to_all x1, blocking collectives, compute(): pieces = lax.all_to_all(summed, ('yhi', 'xh'), 0, 0, tiled=True)  17.4 us
    ppermute x3, waiting for transfers between devices, compute(): have[-step] = lax.ppermute(have[1 - step], ALL, up)  11.7 us
    ppermute x1, waiting for transfers between devices, compute(): lax.ppermute(pair[1], 'xp', [(0, 1), (1, 0)])  8.1 us
    ppermute x3, starting transfers between devices, compute(): have[-step] = lax.ppermute(have[1 - step], ALL, up)  8.09 us
    pallas_call x1, Pallas kernels, split_amplitudes(): pl.pallas_call(split_kernel, grid_spec=pltpu.PrefetchScalarGridSpec(num_s...  5.71 us
    ppermute x1, starting transfers between devices, compute(): last_down = lax.ppermute(have[3][8:], ALL, down)  5.13 us
  transfers between devices with their start and end apart: 13, of which 7 were waited for; matrix products, arithmetic and copies ran while one was open for 0% of the time, Pallas kernels for 2%

commit v1 on v0

--- a/solution.py
+++ b/solution.py
@@ -28,14 +28,17 @@
     return groups
 
 
-def ring_pairs(step):
+def ring_pairs(parity):
+    def partner(at):
+        return (at + 1 if at % 2 == parity else at - 1) % 8
+
     pairs = []
     for xh in range(XH):
         for xp in range(XP):
             for y in range(Y):
                 for z in range(Z):
-                    pairs.append((place(y, z, xh, xp, 0), place(y, (z + step) % Z, xh, xp, 0)))
-                    pairs.append((place(y, z, xh, xp, 1), place((y + step) % Y, z, xh, xp, 1)))
+                    pairs.append((place(y, z, xh, xp, 0), place(y, partner(z), xh, xp, 0)))
+                    pairs.append((place(y, z, xh, xp, 1), place(partner(y), z, xh, xp, 1)))
     return sorted(pairs)
 
 
@@ -63,40 +66,50 @@
     out_ref[...] = jnp.broadcast_to(masked[None], out_ref.shape)
 
 
-def split_kernel(meta, *refs):
-    own, swap, across = refs[2 * TEAM :]
-    outs = (own.at[0], swap.at[0], across.at[0, 0], across.at[1, 0])
-    for values, tiles, out in zip(refs[:TEAM], refs[TEAM : 2 * TEAM], outs, strict=True):
-        flags = spread(tiles[0])
+JOBS = [(n, quad) for n in (2, 3, 0, 1) for quad in range(QUADS)]
+
+
+def split_kernel(meta, amps, tiles, own, swap, across, taken, dealt, load_sem, store_sem):
+    me = meta[3]
+    loads, stores = [], []
+    for job, (n, quad) in enumerate(JOBS):
+        lanes = pl.ds(pl.multiple_of((TEAM * quad + (me ^ n)) * PANEL, PANEL), PANEL)
+        loads.append(pltpu.make_async_copy(amps.at[:, lanes], taken.at[job], load_sem.at[job]))
+        target = (own.at[quad], swap.at[quad], across.at[0, quad], across.at[1, quad])[n]
+        stores.append(pltpu.make_async_copy(dealt.at[job], target, store_sem.at[job]))
+    for load in loads:
+        load.start()
+    for job, (n, quad) in enumerate(JOBS):
+        loads[job].wait()
+        flags = spread(tiles[TEAM * quad + (me ^ n)])
         for part in range(PAIRS // TILE):
             rows = pl.ds(part * TILE, TILE)
-            out[rows, :] = (values[rows, :].astype(jnp.float32) * flags[part : part + 1]).astype(jnp.bfloat16)
-
-
-def split_amplitudes(meta, amplitudes, amp_tiles):
-    tiles = amp_tiles.reshape(PAIRS // TILE, QUADS * TEAM, PANEL // TILE).transpose(1, 0, 2)
-
-    def values(n):
-        return pl.BlockSpec((PAIRS, PANEL), lambda i, m: (0, TEAM * i + (m[3] ^ n)))
-
-    def flags(n):
-        return pl.BlockSpec((1, PAIRS // TILE, PANEL // TILE), lambda i, m: (TEAM * i + (m[3] ^ n), 0, 0))
-
-    block = pl.BlockSpec((1, PAIRS, PANEL), lambda i, m: (i, 0, 0))
+            block = taken[job, rows, :].astype(jnp.float32)
+            dealt[job, rows, :] = (block * flags[part : part + 1]).astype(jnp.bfloat16)
+        if job:
+            stores[job - 1].start()
+    stores[-1].start()
+    for store in stores:
+        store.wait()
+
+
+def split_amplitudes(meta, amplitudes, tiles):
     shape = (QUADS, PAIRS, PANEL)
     return pl.pallas_call(
         split_kernel,
-        grid_spec=pltpu.PrefetchScalarGridSpec(
-            num_scalar_prefetch=1,
-            grid=(QUADS,),
-            in_specs=[values(n) for n in range(TEAM)] + [flags(n) for n in range(TEAM)],
-            out_specs=[block, block, pl.BlockSpec((CORE, 1, PAIRS, PANEL), lambda i, m: (0, i, 0, 0))],
-        ),
+        in_specs=[
+            pl.BlockSpec(memory_space=pltpu.SMEM),
+            pl.BlockSpec(memory_space=pltpu.HBM),
+            pl.BlockSpec(memory_space=pltpu.VMEM),
+        ],
+        out_specs=[pl.BlockSpec(memory_space=pltpu.HBM)] * 3,
         out_shape=[jax.ShapeDtypeStruct(s, jnp.bfloat16) for s in (shape, shape, (CORE,) + shape)],
+        scratch_shapes=[pltpu.VMEM((len(JOBS), PAIRS, PANEL), jnp.bfloat16)] * 2
+        + [pltpu.SemaphoreType.DMA((len(JOBS),))] * 2,
         compiler_params=pltpu.CompilerParams(vmem_limit_bytes=60 << 20),
         cost_estimate=pl.CostEstimate(flops=8 << 20, bytes_accessed=8 << 20, transcendentals=0),
         name="split_amplitudes",
-    )(meta, *[amplitudes] * TEAM, *[tiles] * TEAM)
+    )(meta, amplitudes, tiles)
 
 
 MEMBERS = XH * 8
@@ -108,11 +121,12 @@
     keep_ref, send_ref, ints, amps, total, sem = refs[len(SLOTS) + TEAM :]
     core, here, me = meta[0], meta[1], meta[3]
     xp = me // CORE
+    sign = 1 - 2 * lax.rem(here, 2)
 
     def copies(on):
         found = []
         for source, (offset, first, members) in zip(blocks, SLOTS, strict=True):
-            there = lax.rem(here + offset + 8, 8)
+            there = lax.rem(here + sign * offset + 8, 8)
             for xh in range(first // 8, (first + members) // 8):
                 at = xh * 8 - first
                 if on == 0:
@@ -180,19 +194,20 @@
     )(meta, integrals, int_tiles)
     plane = lax.all_to_all(panels, ALL, 0, 0, axis_index_groups=plane_groups(), tiled=True)
 
-    own, swap, across = split_amplitudes(meta, amplitudes, amp_tiles)
+    tiles = amp_tiles.reshape(PAIRS // TILE, QUADS * TEAM, PANEL // TILE).transpose(1, 0, 2)
+    own, swap, across = split_amplitudes(meta, amplitudes, tiles)
     across = lax.ppermute(across, "xp", [(0, 1), (1, 0)])
     swap = lax.ppermute(swap, "core", [(0, 1), (1, 0)])
     relay = lax.ppermute(across[1], "core", [(0, 1), (1, 0)])
 
-    up, down = ring_pairs(1), ring_pairs(-1)
+    even, odd = ring_pairs(0), ring_pairs(1)
     have = {0: plane}
     for step in (1, 2, 3):
-        have[-step] = lax.ppermute(have[1 - step], ALL, up)
-        have[step] = lax.ppermute(have[step - 1], ALL, down)
-    last_up = lax.ppermute(have[-3][:8], ALL, up)
-    last_down = lax.ppermute(have[3][8:], ALL, down)
-    blocks = [have[offset] for offset, _, _ in SLOTS[:7]] + [last_up, last_down]
+        have[step] = lax.ppermute(have[1 - step], ALL, even)
+        have[-step] = lax.ppermute(have[step - 1], ALL, odd)
+    last_odd = lax.ppermute(have[3][:8], ALL, odd)
+    last_even = lax.ppermute(have[-3][8:], ALL, even)
+    blocks = [have[offset] for offset, _, _ in SLOTS[:7]] + [last_odd, last_even]
 
     share = jax.ShapeDtypeStruct((XP, QUADS, 32, TEAM * PAIRS), jnp.float32)
     keep, send = pl.pallas_call(

time: 156 us -> 156 us (level)
  no operation moved by 1% of the time
where the time goes in v1:
time: 156 us; the launch traced here: 155 us
  blocking collectives  68.8 us (44%)
  starting transfers between devices  45.9 us (29%)
  waiting for transfers between devices  25 us (16%)
  Pallas kernels  12.4 us (8%)
  local copies, waits for them, and re-layouts  2.17 us (1%)
    all_to_all x1, blocking collectives, compute(): lax.all_to_all(panels, ALL, 0, 0, axis_index_groups=plane_groups(), tiled...  51.4 us
    ppermute x3, starting transfers between devices, compute(): have[-step] = lax.ppermute(have[step - 1], ALL, odd)  19.4 us
    all_to_all x1, blocking collectives, compute(): pieces = lax.all_to_all(summed, ('yhi', 'xh'), 0, 0, tiled=True)  17.4 us
    ppermute x3, starting transfers between devices, compute(): have[step] = lax.ppermute(have[1 - step], ALL, even)  8.1 us
    ppermute x1, waiting for transfers between devices, compute(): lax.ppermute(pair[1], 'xp', [(0, 1), (1, 0)])  8.1 us
    ppermute x3, waiting for transfers between devices, compute(): have[step] = lax.ppermute(have[1 - step], ALL, even)  5.49 us
    pallas_call x1, Pallas kernels, split_amplitudes(): pl.pallas_call(split_kernel, in_specs=[pl.BlockSpec(memory_space=pltpu.SM...  5.33 us
    ppermute x1, starting transfers between devices, compute(): last_odd = lax.ppermute(have[3][:8], ALL, odd)  5.13 us
  transfers between devices with their start and end apart: 13, of which 7 were waited for; matrix products, arithmetic and copies ran while one was open for 0% of the time, Pallas kernels for 2%

profile of v1, /device:TPU:8, one launch (start us, length us, event | category | flops | bytes accessed | tf_op | source)
XLA Modules:
  0.0 155.2 jit_solution(13121320801312487479)
XLA Ops:
  0.0 0.8 reshape.6
  0.8 0.6 copy.9
  1.4 0.6 pad_add_fusion.meta
  2.0 5.3 %split_amplitudes.1 = (bf16[4,128,1024]{2,1,0:T(8,128)(2,1)}, bf16[4,128,1024]{2,1,0:T(8,128)(2,1)}, bf16[2,4,128,1024]{3,2,1,0:T(8,128)(2,1)}) custom-call(s32[4]{0:T(128)} %pad_add_fusion.meta, bf16[128,16384]{1,0:T(8,128)(2,1)} %amps.1, s32[16,2,16]{2,1,0:T(2,128)} %bitcast.21), custom_call_target="tpu_custom_call" | custom-call | flops 8388608 | bytes 8388608 | tf_op jit(solution)/shard_map/split_amplitudes/pallas_call | solution.py:98
  7.4 3.4 %collective-permute-start.9 = (bf16[2,4,128,1024]{3,2,1,0:T(8,128)(2,1)}, bf16[2,4,128,1024]{3,2,1,0:T(8,128)(2,1)S(1)}, u32[]{:S(2)}, u32[]{:S(2)}) collective-permute-start(bf16[2,4,128,1024]{3,2,1,0:T(8,128)(2,1)} %get-tuple-element.12), channel_id=1, source_target_pairs={{0,2},{2,0},{1,3},{3,1},{4,6},{6,4},{5,7},{7,5},{8,10},{10,8},{9,1... | collective-permute-start | bytes 6291464 | tf_op jit(solution)/shard_map/ppermute | solution.py:199
  10.8 2.4 %mask_integrals.1 = bf16[16,16,1024]{2,1,0:T(8,128)(2,1)} custom-call(s32[4]{0:T(128)} %pad_add_fusion.meta, bf16[16,1024]{1,0:T(8,128)(2,1)} %ints_hbm.1, s32[8,16]{1,0:T(8,128)} %tiles_hbm.1), custom_call_target="tpu_custom_call" | custom-call | tf_op jit(solution)/shard_map/mask_integrals/pallas_call | solution.py:182
  13.2 0.0 copy-start
  13.2 0.0 copy-start.1
  13.2 51.4 %all_to_all.10.refs_0_ = bf16[16,16,1024]{2,1,0:T(8,128)(2,1)S(1)} all-to-all(bf16[16,16,1024]{2,1,0:T(8,128)(2,1)} %mask_integrals.1), channel_id=1, replica_groups={{0,128,256,384,8,136,264,392,4,132,260,388,12,140,268,396},{16,144,272,..., dimensions={0} | all-to-all | bytes 1048576 | tf_op jit(solution)/shard_map/all_to_all | solution.py:195
  64.6 4.3 %collective-permute-start.1 = (bf16[16,16,1024]{2,1,0:T(8,128)(2,1)S(1)}, bf16[16,16,1024]{2,1,0:T(8,128)(2,1)S(1)}, u32[]{:S(2)}, u32[]{:S(2)}) collective-permute-start(bf16[16,16,1024]{2,1,0:T(8,128)(2,1)S(1)} %all_to_all.10.refs_0_), channel_id=1, source_target_pairs={{0,16},{1,129},{2,18},{3,131},{4,20},{5,133},{6,22},{7,135},{8,24}... | collective-permute-start | bytes 1572872 | tf_op jit(solution)/shard_map/ppermute | solution.py:206
  68.9 9.1 %collective-permute-start = (bf16[16,16,1024]{2,1,0:T(8,128)(2,1)S(1)}, bf16[16,16,1024]{2,1,0:T(8,128)(2,1)S(1)}, u32[]{:S(2)}, u32[]{:S(2)}) collective-permute-start(bf16[16,16,1024]{2,1,0:T(8,128)(2,1)S(1)} %all_to_all.10.refs_0_), channel_id=1, source_target_pairs={{0,112},{1,393},{2,114},{3,395},{4,116},{5,397},{6,118},{7,399},{8... | collective-permute-start | bytes 1572872 | tf_op jit(solution)/shard_map/ppermute | solution.py:207
  78.1 1.9 %collective-permute-start.8 = (bf16[4,128,1024]{2,1,0:T(8,128)(2,1)}, bf16[4,128,1024]{2,1,0:T(8,128)(2,1)S(1)}, u32[]{:S(2)}, u32[]{:S(2)}) collective-permute-start(bf16[4,128,1024]{2,1,0:T(8,128)(2,1)} %get-tuple-element.11), channel_id=1, source_target_pairs={{0,1},{1,0},{2,3},{3,2},{4,5},{5,4},{6,7},{7,6},{8,9},{9,8},{10,11... | collective-permute-start | bytes 3145736 | tf_op jit(solution)/shard_map/ppermute | solution.py:200
  80.0 0.0 collective-permute-done.1.refs_2_
  80.0 6.6 %collective-permute-start.2 = (bf16[16,16,1024]{2,1,0:T(8,128)(2,1)S(1)}, bf16[16,16,1024]{2,1,0:T(8,128)(2,1)S(1)}, u32[]{:S(2)}, u32[]{:S(2)}) collective-permute-start(bf16[16,16,1024]{2,1,0:T(8,128)(2,1)S(1)} %collective-permute-done.1.refs_2_), channel_id=1, source_target_pairs={{0,112},{1,393},{2,114},{3,395},{4,116},{5,397},{6,118},{7,399},{8... | collective-permute-start | bytes 1572872 | tf_op jit(solution)/shard_map/ppermute | solution.py:207
  86.6 0.0 collective-permute-done.refs_1_
  86.7 1.9 %collective-permute-start.3 = (bf16[16,16,1024]{2,1,0:T(8,128)(2,1)S(1)}, bf16[16,16,1024]{2,1,0:T(8,128)(2,1)S(1)}, u32[]{:S(2)}, u32[]{:S(2)}) collective-permute-start(bf16[16,16,1024]{2,1,0:T(8,128)(2,1)S(1)} %collective-permute-done.refs_1_), channel_id=1, source_target_pairs={{0,16},{1,129},{2,18},{3,131},{4,20},{5,133},{6,22},{7,135},{8,24}... | collective-permute-start | bytes 1572872 | tf_op jit(solution)/shard_map/ppermute | solution.py:206
  88.6 0.0 collective-permute-done.9.refs_11_
  88.6 0.1 slice_bitcast_fusion
  88.7 1.9 %collective-permute-start.10 = (bf16[4,128,1024]{2,1,0:T(8,128)(2,1)S(1)}, bf16[4,128,1024]{2,1,0:T(8,128)(2,1)S(1)}, u32[]{:S(2)}, u32[]{:S(2)}) collective-permute-start(bf16[4,128,1024]{2,1,0:T(8,128)(2,1)S(1)} %slice_bitcast_fusion), channel_id=1, source_target_pairs={{0,1},{1,0},{2,3},{3,2},{4,5},{5,4},{6,7},{7,6},{8,9},{9,8},{10,11... | collective-permute-start | bytes 3145736 | tf_op jit(solution)/shard_map/ppermute | solution.py:201
  90.6 3.2 %collective-permute-done.2.refs_3_ = bf16[16,16,1024]{2,1,0:T(8,128)(2,1)S(1)} collective-permute-done((bf16[16,16,1024]{2,1,0:T(8,128)(2,1)S(1)}, bf16[16,16,1024]{2,1,0:T(8,128)(2,1)S(1)}, u32[]{:S(2)}, u32[]{:S(2)}) %collective-permute-start.2) | collective-permute-done | bytes 524320 | tf_op jit(solution)/shard_map/ppermute | solution.py:207
  93.8 1.9 %collective-permute-start.5 = (bf16[16,16,1024]{2,1,0:T(8,128)(2,1)S(1)}, bf16[16,16,1024]{2,1,0:T(8,128)(2,1)S(1)}, u32[]{:S(2)}, u32[]{:S(2)}) collective-permute-start(bf16[16,16,1024]{2,1,0:T(8,128)(2,1)S(1)} %collective-permute-done.2.refs_3_), channel_id=1, source_target_pairs={{0,16},{1,129},{2,18},{3,131},{4,20},{5,133},{6,22},{7,135},{8,24}... | collective-permute-start | bytes 1572872 | tf_op jit(solution)/shard_map/ppermute | solution.py:206
  95.7 2.0 %collective-permute-done.3.refs_4_ = bf16[16,16,1024]{2,1,0:T(8,128)(2,1)S(1)} collective-permute-done((bf16[16,16,1024]{2,1,0:T(8,128)(2,1)S(1)}, bf16[16,16,1024]{2,1,0:T(8,128)(2,1)S(1)}, u32[]{:S(2)}, u32[]{:S(2)}) %collective-permute-start.3) | collective-permute-done | bytes 524320 | tf_op jit(solution)/shard_map/ppermute | solution.py:206
  97.7 3.6 %collective-permute-start.4 = (bf16[16,16,1024]{2,1,0:T(8,128)(2,1)S(1)}, bf16[16,16,1024]{2,1,0:T(8,128)(2,1)S(1)}, u32[]{:S(2)}, u32[]{:S(2)}) collective-permute-start(bf16[16,16,1024]{2,1,0:T(8,128)(2,1)S(1)} %collective-permute-done.3.refs_4_), channel_id=1, source_target_pairs={{0,112},{1,393},{2,114},{3,395},{4,116},{5,397},{6,118},{7,399},{8... | collective-permute-start | bytes 1572872 | tf_op jit(solution)/shard_map/ppermute | solution.py:207
  101.4 3.5 %collective-permute-done.5.refs_6_ = bf16[16,16,1024]{2,1,0:T(8,128)(2,1)S(1)} collective-permute-done((bf16[16,16,1024]{2,1,0:T(8,128)(2,1)S(1)}, bf16[16,16,1024]{2,1,0:T(8,128)(2,1)S(1)}, u32[]{:S(2)}, u32[]{:S(2)}) %collective-permute-start.5) | collective-permute-done | bytes 524320 | tf_op jit(solution)/shard_map/ppermute | solution.py:206
  104.9 5.1 %collective-permute-start.6 = (bf16[8,16,1024]{2,1,0:T(8,128)(2,1)S(1)}, bf16[8,16,1024]{2,1,0:T(8,128)(2,1)S(1)}, u32[]{:S(2)}, u32[]{:S(2)}) collective-permute-start(bf16[8,16,1024]{2,1,0:T(8,128)(2,1)S(1)} %slice.20), channel_id=1, source_target_pairs={{0,112},{1,393},{2,114},{3,395},{4,116},{5,397},{6,118},{7,399},{8... | collective-permute-start | bytes 786440 | tf_op jit(solution)/shard_map/ppermute | solution.py:208
  110.0 0.0 collective-permute-done.4.refs_5_
  110.1 1.9 %collective-permute-start.7 = (bf16[8,16,1024]{2,1,0:T(8,128)(2,1)S(1)}, bf16[8,16,1024]{2,1,0:T(8,128)(2,1)S(1)}, u32[]{:S(2)}, u32[]{:S(2)}) collective-permute-start(bf16[8,16,1024]{2,1,0:T(8,128)(2,1)S(1)} %slice.21), channel_id=1, source_target_pairs={{0,16},{1,129},{2,18},{3,131},{4,20},{5,133},{6,22},{7,135},{8,24}... | collective-permute-start | bytes 786440 | tf_op jit(solution)/shard_map/ppermute | solution.py:209
  112.0 0.0 collective-permute-done.8.refs_10_
  112.0 2.4 %collective-permute-done.6.refs_7_ = bf16[8,16,1024]{2,1,0:T(8,128)(2,1)S(1)} collective-permute-done((bf16[8,16,1024]{2,1,0:T(8,128)(2,1)S(1)}, bf16[8,16,1024]{2,1,0:T(8,128)(2,1)S(1)}, u32[]{:S(2)}, u32[]{:S(2)}) %collective-permute-start.6) | collective-permute-done | bytes 262176 | tf_op jit(solution)/shard_map/ppermute | solution.py:208
  114.4 4.0 %collective-permute-done.7.refs_8_ = bf16[8,16,1024]{2,1,0:T(8,128)(2,1)S(1)} collective-permute-done((bf16[8,16,1024]{2,1,0:T(8,128)(2,1)S(1)}, bf16[8,16,1024]{2,1,0:T(8,128)(2,1)S(1)}, u32[]{:S(2)}, u32[]{:S(2)}) %collective-permute-start.7) | collective-permute-done | bytes 262176 | tf_op jit(solution)/shard_map/ppermute | solution.py:209
  118.3 0.0 collective-permute-done.10.refs_12_
  118.3 0.0 copy-done
  118.3 0.0 copy-done.1
  118.3 4.7 %ladder.1 = (f32[2,4,32,512]{3,2,1,0:T(8,128)S(1)}, f32[2,4,32,512]{3,2,1,0:T(8,128)S(1)}) custom-call(s32[4]{0:T(128)S(1)} %copy-done.1, bf16[16,16,1024]{2,1,0:T(8,128)(2,1)S(1)} %all_to_all.10.refs_0_, bf16[16,16,1024]{2,1,0:T(8,128)(2,1)S(1)} %collective-permute-done.refs_1_, bf16[16,16,1024]{2,1,0:T(8,128)(2,1)S(1)} %collective-permute-done.1.refs_2_, ...), custom_call_target="tpu_custom_call" | custom-call | flops 2147483648 | bytes 10485760 | tf_op jit(solution)/shard_map/ladder/pallas_call | solution.py:213
  123.0 1.9 %collective-permute-start.11 = (f32[2,4,32,512]{3,2,1,0:T(8,128)S(1)}, f32[2,4,32,512]{3,2,1,0:T(8,128)S(1)}, u32[]{:S(2)}, u32[]{:S(2)}) collective-permute-start(f32[2,4,32,512]{3,2,1,0:T(8,128)S(1)} %get-tuple-element.14), channel_id=1, source_target_pairs={{0,1},{1,0},{2,3},{3,2},{4,5},{5,4},{6,7},{7,6},{8,9},{9,8},{10,11... | collective-permute-start | bytes 1572872 | tf_op jit(solution)/shard_map/ppermute | solution.py:229
  124.9 1.9 %collective-permute-done.11 = f32[2,4,32,512]{3,2,1,0:T(8,128)S(1)} collective-permute-done((f32[2,4,32,512]{3,2,1,0:T(8,128)S(1)}, f32[2,4,32,512]{3,2,1,0:T(8,128)S(1)}, u32[]{:S(2)}, u32[]{:S(2)}) %collective-permute-start.11) | collective-permute-done | bytes 524320 | tf_op jit(solution)/shard_map/ppermute | solution.py:229
  126.8 0.1 add.19
  126.9 2.1 %collective-permute-start.12 = (f32[4,32,512]{2,1,0:T(8,128)S(1)}, f32[4,32,512]{2,1,0:T(8,128)S(1)}, u32[]{:S(2)}, u32[]{:S(2)}) collective-permute-start(f32[4,32,512]{2,1,0:T(8,128)S(1)} %slice_bitcast_fusion.1), channel_id=1, source_target_pairs={{0,2},{2,0},{1,3},{3,1},{4,6},{6,4},{5,7},{7,5},{8,10},{10,8},{9,1... | collective-permute-start | bytes 786440 | tf_op jit(solution)/shard_map/ppermute | solution.py:230
  129.1 8.1 %collective-permute-done.12 = f32[4,32,512]{2,1,0:T(8,128)S(1)} collective-permute-done((f32[4,32,512]{2,1,0:T(8,128)S(1)}, f32[4,32,512]{2,1,0:T(8,128)S(1)}, u32[]{:S(2)}, u32[]{:S(2)}) %collective-permute-start.12) | collective-permute-done | bytes 262176 | tf_op jit(solution)/shard_map/ppermute | solution.py:230
  137.2 17.4 %all_to_all.11 = bf16[4,32,512]{2,1,0:T(8,128)(2,1)S(1)} all-to-all(bf16[4,32,512]{2,1,0:T(8,128)(2,1)S(1)} %fusion.1), channel_id=1, replica_groups=mesh['ylo'=4,'z'=8,'yhi'=2,'xh'=2,'xp'=2,'core'=2] {'yhi','xh'}, dimensions={0} | all-to-all | bytes 262144 | tf_op jit(solution)/shard_map/all_to_all | solution.py:231
  154.6 0.7 copy.7
  (4 shorter events, 0.1 us)
Async XLA Ops:
  7.4 81.2 %collective-permute-start.9 = (bf16[2,4,128,1024]{3,2,1,0:T(8,128)(2,1)}, bf16[2,4,128,1024]{3,2,1,0:T(8,128)(2,1)S(1)}, u32[]{:S(2)}, u32[]{:S(2)}) collective-permute-start(bf16[2,4,128,1024]{3,2,1,0:T(8,128)(2,1)} %get-tuple-element.12), channel_id=1, source_target_pairs={{0,2},{2,0},{1,3},{3,1},{4,6},{6,4},{5,7},{7,5},{8,10},{10,8},{9,1... | collective-permute-start | bytes 6291464 | tf_op jit(solution)/shard_map/ppermute | solution.py:199
  13.2 105.1 %copy-start = (bf16[4,128,1024]{2,1,0:T(8,128)(2,1)S(1)}, bf16[4,128,1024]{2,1,0:T(8,128)(2,1)}, u32[]{:S(2)}) copy-start(bf16[4,128,1024]{2,1,0:T(8,128)(2,1)} %get-tuple-element.10.refs_9_) | copy-start | bytes 3145732
  13.2 105.1 %copy-start.1 = (s32[4]{0:T(128)S(1)}, s32[4]{0:T(128)}, u32[]{:S(2)}) copy-start(s32[4]{0:T(128)} %pad_add_fusion.meta) | copy-start | bytes 52
  64.6 15.3 %collective-permute-start.1 = (bf16[16,16,1024]{2,1,0:T(8,128)(2,1)S(1)}, bf16[16,16,1024]{2,1,0:T(8,128)(2,1)S(1)}, u32[]{:S(2)}, u32[]{:S(2)}) collective-permute-start(bf16[16,16,1024]{2,1,0:T(8,128)(2,1)S(1)} %all_to_all.10.refs_0_), channel_id=1, source_target_pairs={{0,16},{1,129},{2,18},{3,131},{4,20},{5,133},{6,22},{7,135},{8,24}... | collective-permute-start | bytes 1572872 | tf_op jit(solution)/shard_map/ppermute | solution.py:206
  68.9 17.7 %collective-permute-start = (bf16[16,16,1024]{2,1,0:T(8,128)(2,1)S(1)}, bf16[16,16,1024]{2,1,0:T(8,128)(2,1)S(1)}, u32[]{:S(2)}, u32[]{:S(2)}) collective-permute-start(bf16[16,16,1024]{2,1,0:T(8,128)(2,1)S(1)} %all_to_all.10.refs_0_), channel_id=1, source_target_pairs={{0,112},{1,393},{2,114},{3,395},{4,116},{5,397},{6,118},{7,399},{8... | collective-permute-start | bytes 1572872 | tf_op jit(solution)/shard_map/ppermute | solution.py:207
  78.1 33.9 %collective-permute-start.8 = (bf16[4,128,1024]{2,1,0:T(8,128)(2,1)}, bf16[4,128,1024]{2,1,0:T(8,128)(2,1)S(1)}, u32[]{:S(2)}, u32[]{:S(2)}) collective-permute-start(bf16[4,128,1024]{2,1,0:T(8,128)(2,1)} %get-tuple-element.11), channel_id=1, source_target_pairs={{0,1},{1,0},{2,3},{3,2},{4,5},{5,4},{6,7},{7,6},{8,9},{9,8},{10,11... | collective-permute-start | bytes 3145736 | tf_op jit(solution)/shard_map/ppermute | solution.py:200
  80.0 13.8 %collective-permute-start.2 = (bf16[16,16,1024]{2,1,0:T(8,128)(2,1)S(1)}, bf16[16,16,1024]{2,1,0:T(8,128)(2,1)S(1)}, u32[]{:S(2)}, u32[]{:S(2)}) collective-permute-start(bf16[16,16,1024]{2,1,0:T(8,128)(2,1)S(1)} %collective-permute-done.1.refs_2_), channel_id=1, source_target_pairs={{0,112},{1,393},{2,114},{3,395},{4,116},{5,397},{6,118},{7,399},{8... | collective-permute-start | bytes 1572872 | tf_op jit(solution)/shard_map/ppermute | solution.py:207
  86.7 11.1 %collective-permute-start.3 = (bf16[16,16,1024]{2,1,0:T(8,128)(2,1)S(1)}, bf16[16,16,1024]{2,1,0:T(8,128)(2,1)S(1)}, u32[]{:S(2)}, u32[]{:S(2)}) collective-permute-start(bf16[16,16,1024]{2,1,0:T(8,128)(2,1)S(1)} %collective-permute-done.refs_1_), channel_id=1, source_target_pairs={{0,16},{1,129},{2,18},{3,131},{4,20},{5,133},{6,22},{7,135},{8,24}... | collective-permute-start | bytes 1572872 | tf_op jit(solution)/shard_map/ppermute | solution.py:206
  88.7 29.6 %collective-permute-start.10 = (bf16[4,128,1024]{2,1,0:T(8,128)(2,1)S(1)}, bf16[4,128,1024]{2,1,0:T(8,128)(2,1)S(1)}, u32[]{:S(2)}, u32[]{:S(2)}) collective-permute-start(bf16[4,128,1024]{2,1,0:T(8,128)(2,1)S(1)} %slice_bitcast_fusion), channel_id=1, source_target_pairs={{0,1},{1,0},{2,3},{3,2},{4,5},{5,4},{6,7},{7,6},{8,9},{9,8},{10,11... | collective-permute-start | bytes 3145736 | tf_op jit(solution)/shard_map/ppermute | solution.py:201
  93.8 11.1 %collective-permute-start.5 = (bf16[16,16,1024]{2,1,0:T(8,128)(2,1)S(1)}, bf16[16,16,1024]{2,1,0:T(8,128)(2,1)S(1)}, u32[]{:S(2)}, u32[]{:S(2)}) collective-permute-start(bf16[16,16,1024]{2,1,0:T(8,128)(2,1)S(1)} %collective-permute-done.2.refs_3_), channel_id=1, source_target_pairs={{0,16},{1,129},{2,18},{3,131},{4,20},{5,133},{6,22},{7,135},{8,24}... | collective-permute-start | bytes 1572872 | tf_op jit(solution)/shard_map/ppermute | solution.py:206
  97.7 12.3 %collective-permute-start.4 = (bf16[16,16,1024]{2,1,0:T(8,128)(2,1)S(1)}, bf16[16,16,1024]{2,1,0:T(8,128)(2,1)S(1)}, u32[]{:S(2)}, u32[]{:S(2)}) collective-permute-start(bf16[16,16,1024]{2,1,0:T(8,128)(2,1)S(1)} %collective-permute-done.3.refs_4_), channel_id=1, source_target_pairs={{0,112},{1,393},{2,114},{3,395},{4,116},{5,397},{6,118},{7,399},{8... | collective-permute-start | bytes 1572872 | tf_op jit(solution)/shard_map/ppermute | solution.py:207
  104.9 9.5 %collective-permute-start.6 = (bf16[8,16,1024]{2,1,0:T(8,128)(2,1)S(1)}, bf16[8,16,1024]{2,1,0:T(8,128)(2,1)S(1)}, u32[]{:S(2)}, u32[]{:S(2)}) collective-permute-start(bf16[8,16,1024]{2,1,0:T(8,128)(2,1)S(1)} %slice.20), channel_id=1, source_target_pairs={{0,112},{1,393},{2,114},{3,395},{4,116},{5,397},{6,118},{7,399},{8... | collective-permute-start | bytes 786440 | tf_op jit(solution)/shard_map/ppermute | solution.py:208
  110.1 8.3 %collective-permute-start.7 = (bf16[8,16,1024]{2,1,0:T(8,128)(2,1)S(1)}, bf16[8,16,1024]{2,1,0:T(8,128)(2,1)S(1)}, u32[]{:S(2)}, u32[]{:S(2)}) collective-permute-start(bf16[8,16,1024]{2,1,0:T(8,128)(2,1)S(1)} %slice.21), channel_id=1, source_target_pairs={{0,16},{1,129},{2,18},{3,131},{4,20},{5,133},{6,22},{7,135},{8,24}... | collective-permute-start | bytes 786440 | tf_op jit(solution)/shard_map/ppermute | solution.py:209
  123.0 3.8 %collective-permute-start.11 = (f32[2,4,32,512]{3,2,1,0:T(8,128)S(1)}, f32[2,4,32,512]{3,2,1,0:T(8,128)S(1)}, u32[]{:S(2)}, u32[]{:S(2)}) collective-permute-start(f32[2,4,32,512]{3,2,1,0:T(8,128)S(1)} %get-tuple-element.14), channel_id=1, source_target_pairs={{0,1},{1,0},{2,3},{3,2},{4,5},{5,4},{6,7},{7,6},{8,9},{9,8},{10,11... | collective-permute-start | bytes 1572872 | tf_op jit(solution)/shard_map/ppermute | solution.py:229
  126.9 10.2 %collective-permute-start.12 = (f32[4,32,512]{2,1,0:T(8,128)S(1)}, f32[4,32,512]{2,1,0:T(8,128)S(1)}, u32[]{:S(2)}, u32[]{:S(2)}) collective-permute-start(f32[4,32,512]{2,1,0:T(8,128)S(1)} %slice_bitcast_fusion.1), channel_id=1, source_target_pairs={{0,2},{2,0},{1,3},{3,1},{4,6},{6,4},{5,7},{7,5},{8,10},{10,8},{9,1... | collective-permute-start | bytes 786440 | tf_op jit(solution)/shard_map/ppermute | solution.py:230

commit v2 on v1

--- a/solution.py
+++ b/solution.py
@@ -79,9 +79,12 @@
         stores.append(pltpu.make_async_copy(dealt.at[job], target, store_sem.at[job]))
     for load in loads:
         load.start()
+    width = tiles.shape[1]
+    known = jnp.concatenate([tiles[...]] * 4, axis=0)
     for job, (n, quad) in enumerate(JOBS):
         loads[job].wait()
-        flags = spread(tiles[TEAM * quad + (me ^ n)])
+        first = (TEAM * quad + (me ^ n)) * (PANEL // TILE)
+        flags = spread(pltpu.roll(known, lax.rem(width - first, width), 1)[:, : PANEL // TILE])
         for part in range(PAIRS // TILE):
             rows = pl.ds(part * TILE, TILE)
             block = taken[job, rows, :].astype(jnp.float32)
@@ -194,8 +197,7 @@
     )(meta, integrals, int_tiles)
     plane = lax.all_to_all(panels, ALL, 0, 0, axis_index_groups=plane_groups(), tiled=True)
 
-    tiles = amp_tiles.reshape(PAIRS // TILE, QUADS * TEAM, PANEL // TILE).transpose(1, 0, 2)
-    own, swap, across = split_amplitudes(meta, amplitudes, tiles)
+    own, swap, across = split_amplitudes(meta, amplitudes, amp_tiles)
     across = lax.ppermute(across, "xp", [(0, 1), (1, 0)])
     swap = lax.ppermute(swap, "core", [(0, 1), (1, 0)])
     relay = lax.ppermute(across[1], "core", [(0, 1), (1, 0)])

time: 156 us -> 156 us (level)
  no operation moved by 1% of the time
where the time goes in v2:
time: 156 us; the launch traced here: 155 us
  blocking collectives  68.8 us (44%)
  starting transfers between devices  45.9 us (29%)
  waiting for transfers between devices  25 us (16%)
  Pallas kernels  13.6 us (9%)
    all_to_all x1, blocking collectives, compute(): lax.all_to_all(panels, ALL, 0, 0, axis_index_groups=plane_groups(), tiled...  51.4 us
    ppermute x3, starting transfers between devices, compute(): have[-step] = lax.ppermute(have[step - 1], ALL, odd)  19.4 us
    all_to_all x1, blocking collectives, compute(): pieces = lax.all_to_all(summed, ('yhi', 'xh'), 0, 0, tiled=True)  17.4 us
    ppermute x1, waiting for transfers between devices, compute(): lax.ppermute(pair[1], 'xp', [(0, 1), (1, 0)])  8.1 us
    ppermute x3, starting transfers between devices, compute(): have[step] = lax.ppermute(have[1 - step], ALL, even)  8.1 us
    pallas_call x1, Pallas kernels, split_amplitudes(): pl.pallas_call(split_kernel, in_specs=[pl.BlockSpec(memory_space=pltpu.SM...  6.47 us
    ppermute x3, waiting for transfers between devices, compute(): have[step] = lax.ppermute(have[1 - step], ALL, even)  5.49 us
    ppermute x1, starting transfers between devices, compute(): last_odd = lax.ppermute(have[3][:8], ALL, odd)  5.13 us
  transfers between devices with their start and end apart: 13, of which 7 were waited for; matrix products, arithmetic and copies ran while one was open for 0% of the time, Pallas kernels for 2%

profile of v2, /device:TPU:8, one launch (start us, length us, event | category | flops | bytes accessed | tf_op | source)
XLA Modules:
  0.0 155.0 jit_solution(3152760608732082323)
XLA Ops:
  0.0 0.6 pad_add_fusion.meta
  0.6 6.5 %split_amplitudes.1 = (bf16[4,128,1024]{2,1,0:T(8,128)(2,1)}, bf16[4,128,1024]{2,1,0:T(8,128)(2,1)}, bf16[2,4,128,1024]{3,2,1,0:T(8,128)(2,1)}) custom-call(s32[4]{0:T(128)} %pad_add_fusion.meta, bf16[128,16384]{1,0:T(8,128)(2,1)} %amps.1, s32[2,256]{1,0:T(2,128)} %tiles.1), custom_call_target="tpu_custom_call" | custom-call | flops 8388608 | bytes 8388608 | tf_op jit(solution)/shard_map/split_amplitudes/pallas_call | solution.py:101
  7.1 3.4 %collective-permute-start.9 = (bf16[2,4,128,1024]{3,2,1,0:T(8,128)(2,1)}, bf16[2,4,128,1024]{3,2,1,0:T(8,128)(2,1)S(1)}, u32[]{:S(2)}, u32[]{:S(2)}) collective-permute-start(bf16[2,4,128,1024]{3,2,1,0:T(8,128)(2,1)} %get-tuple-element.12), channel_id=1, source_target_pairs={{0,2},{2,0},{1,3},{3,1},{4,6},{6,4},{5,7},{7,5},{8,10},{10,8},{9,1... | collective-permute-start | bytes 6291464 | tf_op jit(solution)/shard_map/ppermute | solution.py:201
  10.5 2.4 %mask_integrals.1 = bf16[16,16,1024]{2,1,0:T(8,128)(2,1)} custom-call(s32[4]{0:T(128)} %pad_add_fusion.meta, bf16[16,1024]{1,0:T(8,128)(2,1)} %ints_hbm.1, s32[8,16]{1,0:T(8,128)} %tiles_hbm.1), custom_call_target="tpu_custom_call" | custom-call | tf_op jit(solution)/shard_map/mask_integrals/pallas_call | solution.py:185
  13.0 0.0 copy-start
  13.0 0.0 copy-start.1
  13.0 51.4 %all_to_all.10.refs_0_ = bf16[16,16,1024]{2,1,0:T(8,128)(2,1)S(1)} all-to-all(bf16[16,16,1024]{2,1,0:T(8,128)(2,1)} %mask_integrals.1), channel_id=1, replica_groups={{0,128,256,384,8,136,264,392,4,132,260,388,12,140,268,396},{16,144,272,..., dimensions={0} | all-to-all | bytes 1048576 | tf_op jit(solution)/shard_map/all_to_all | solution.py:198
  64.4 4.3 %collective-permute-start.1 = (bf16[16,16,1024]{2,1,0:T(8,128)(2,1)S(1)}, bf16[16,16,1024]{2,1,0:T(8,128)(2,1)S(1)}, u32[]{:S(2)}, u32[]{:S(2)}) collective-permute-start(bf16[16,16,1024]{2,1,0:T(8,128)(2,1)S(1)} %all_to_all.10.refs_0_), channel_id=1, source_target_pairs={{0,16},{1,129},{2,18},{3,131},{4,20},{5,133},{6,22},{7,135},{8,24}... | collective-permute-start | bytes 1572872 | tf_op jit(solution)/shard_map/ppermute | solution.py:208
  68.7 9.1 %collective-permute-start = (bf16[16,16,1024]{2,1,0:T(8,128)(2,1)S(1)}, bf16[16,16,1024]{2,1,0:T(8,128)(2,1)S(1)}, u32[]{:S(2)}, u32[]{:S(2)}) collective-permute-start(bf16[16,16,1024]{2,1,0:T(8,128)(2,1)S(1)} %all_to_all.10.refs_0_), channel_id=1, source_target_pairs={{0,112},{1,393},{2,114},{3,395},{4,116},{5,397},{6,118},{7,399},{8... | collective-permute-start | bytes 1572872 | tf_op jit(solution)/shard_map/ppermute | solution.py:209
  77.8 1.9 %collective-permute-start.8 = (bf16[4,128,1024]{2,1,0:T(8,128)(2,1)}, bf16[4,128,1024]{2,1,0:T(8,128)(2,1)S(1)}, u32[]{:S(2)}, u32[]{:S(2)}) collective-permute-start(bf16[4,128,1024]{2,1,0:T(8,128)(2,1)} %get-tuple-element.11), channel_id=1, source_target_pairs={{0,1},{1,0},{2,3},{3,2},{4,5},{5,4},{6,7},{7,6},{8,9},{9,8},{10,11... | collective-permute-start | bytes 3145736 | tf_op jit(solution)/shard_map/ppermute | solution.py:202
  79.8 0.0 collective-permute-done.1.refs_2_
  79.8 6.6 %collective-permute-start.2 = (bf16[16,16,1024]{2,1,0:T(8,128)(2,1)S(1)}, bf16[16,16,1024]{2,1,0:T(8,128)(2,1)S(1)}, u32[]{:S(2)}, u32[]{:S(2)}) collective-permute-start(bf16[16,16,1024]{2,1,0:T(8,128)(2,1)S(1)} %collective-permute-done.1.refs_2_), channel_id=1, source_target_pairs={{0,112},{1,393},{2,114},{3,395},{4,116},{5,397},{6,118},{7,399},{8... | collective-permute-start | bytes 1572872 | tf_op jit(solution)/shard_map/ppermute | solution.py:209
  86.4 0.0 collective-permute-done.refs_1_
  86.4 1.9 %collective-permute-start.3 = (bf16[16,16,1024]{2,1,0:T(8,128)(2,1)S(1)}, bf16[16,16,1024]{2,1,0:T(8,128)(2,1)S(1)}, u32[]{:S(2)}, u32[]{:S(2)}) collective-permute-start(bf16[16,16,1024]{2,1,0:T(8,128)(2,1)S(1)} %collective-permute-done.refs_1_), channel_id=1, source_target_pairs={{0,16},{1,129},{2,18},{3,131},{4,20},{5,133},{6,22},{7,135},{8,24}... | collective-permute-start | bytes 1572872 | tf_op jit(solution)/shard_map/ppermute | solution.py:208
  88.4 0.0 collective-permute-done.9.refs_11_
  88.4 0.1 slice_bitcast_fusion
  88.4 1.9 %collective-permute-start.10 = (bf16[4,128,1024]{2,1,0:T(8,128)(2,1)S(1)}, bf16[4,128,1024]{2,1,0:T(8,128)(2,1)S(1)}, u32[]{:S(2)}, u32[]{:S(2)}) collective-permute-start(bf16[4,128,1024]{2,1,0:T(8,128)(2,1)S(1)} %slice_bitcast_fusion), channel_id=1, source_target_pairs={{0,1},{1,0},{2,3},{3,2},{4,5},{5,4},{6,7},{7,6},{8,9},{9,8},{10,11... | collective-permute-start | bytes 3145736 | tf_op jit(solution)/shard_map/ppermute | solution.py:203
  90.4 3.2 %collective-permute-done.2.refs_3_ = bf16[16,16,1024]{2,1,0:T(8,128)(2,1)S(1)} collective-permute-done((bf16[16,16,1024]{2,1,0:T(8,128)(2,1)S(1)}, bf16[16,16,1024]{2,1,0:T(8,128)(2,1)S(1)}, u32[]{:S(2)}, u32[]{:S(2)}) %collective-permute-start.2) | collective-permute-done | bytes 524320 | tf_op jit(solution)/shard_map/ppermute | solution.py:209
  93.6 1.9 %collective-permute-start.5 = (bf16[16,16,1024]{2,1,0:T(8,128)(2,1)S(1)}, bf16[16,16,1024]{2,1,0:T(8,128)(2,1)S(1)}, u32[]{:S(2)}, u32[]{:S(2)}) collective-permute-start(bf16[16,16,1024]{2,1,0:T(8,128)(2,1)S(1)} %collective-permute-done.2.refs_3_), channel_id=1, source_target_pairs={{0,16},{1,129},{2,18},{3,131},{4,20},{5,133},{6,22},{7,135},{8,24}... | collective-permute-start | bytes 1572872 | tf_op jit(solution)/shard_map/ppermute | solution.py:208
  95.5 2.0 %collective-permute-done.3.refs_4_ = bf16[16,16,1024]{2,1,0:T(8,128)(2,1)S(1)} collective-permute-done((bf16[16,16,1024]{2,1,0:T(8,128)(2,1)S(1)}, bf16[16,16,1024]{2,1,0:T(8,128)(2,1)S(1)}, u32[]{:S(2)}, u32[]{:S(2)}) %collective-permute-start.3) | collective-permute-done | bytes 524320 | tf_op jit(solution)/shard_map/ppermute | solution.py:208
  97.5 3.6 %collective-permute-start.4 = (bf16[16,16,1024]{2,1,0:T(8,128)(2,1)S(1)}, bf16[16,16,1024]{2,1,0:T(8,128)(2,1)S(1)}, u32[]{:S(2)}, u32[]{:S(2)}) collective-permute-start(bf16[16,16,1024]{2,1,0:T(8,128)(2,1)S(1)} %collective-permute-done.3.refs_4_), channel_id=1, source_target_pairs={{0,112},{1,393},{2,114},{3,395},{4,116},{5,397},{6,118},{7,399},{8... | collective-permute-start | bytes 1572872 | tf_op jit(solution)/shard_map/ppermute | solution.py:209
  101.2 3.5 %collective-permute-done.5.refs_6_ = bf16[16,16,1024]{2,1,0:T(8,128)(2,1)S(1)} collective-permute-done((bf16[16,16,1024]{2,1,0:T(8,128)(2,1)S(1)}, bf16[16,16,1024]{2,1,0:T(8,128)(2,1)S(1)}, u32[]{:S(2)}, u32[]{:S(2)}) %collective-permute-start.5) | collective-permute-done | bytes 524320 | tf_op jit(solution)/shard_map/ppermute | solution.py:208
  104.7 5.1 %collective-permute-start.6 = (bf16[8,16,1024]{2,1,0:T(8,128)(2,1)S(1)}, bf16[8,16,1024]{2,1,0:T(8,128)(2,1)S(1)}, u32[]{:S(2)}, u32[]{:S(2)}) collective-permute-start(bf16[8,16,1024]{2,1,0:T(8,128)(2,1)S(1)} %slice.20), channel_id=1, source_target_pairs={{0,112},{1,393},{2,114},{3,395},{4,116},{5,397},{6,118},{7,399},{8... | collective-permute-start | bytes 786440 | tf_op jit(solution)/shard_map/ppermute | solution.py:210
  109.8 0.0 collective-permute-done.4.refs_5_
  109.8 1.9 %collective-permute-start.7 = (bf16[8,16,1024]{2,1,0:T(8,128)(2,1)S(1)}, bf16[8,16,1024]{2,1,0:T(8,128)(2,1)S(1)}, u32[]{:S(2)}, u32[]{:S(2)}) collective-permute-start(bf16[8,16,1024]{2,1,0:T(8,128)(2,1)S(1)} %slice.21), channel_id=1, source_target_pairs={{0,16},{1,129},{2,18},{3,131},{4,20},{5,133},{6,22},{7,135},{8,24}... | collective-permute-start | bytes 786440 | tf_op jit(solution)/shard_map/ppermute | solution.py:211
  111.8 0.0 collective-permute-done.8.refs_10_
  111.8 2.4 %collective-permute-done.6.refs_7_ = bf16[8,16,1024]{2,1,0:T(8,128)(2,1)S(1)} collective-permute-done((bf16[8,16,1024]{2,1,0:T(8,128)(2,1)S(1)}, bf16[8,16,1024]{2,1,0:T(8,128)(2,1)S(1)}, u32[]{:S(2)}, u32[]{:S(2)}) %collective-permute-start.6) | collective-permute-done | bytes 262176 | tf_op jit(solution)/shard_map/ppermute | solution.py:210
  114.1 4.0 %collective-permute-done.7.refs_8_ = bf16[8,16,1024]{2,1,0:T(8,128)(2,1)S(1)} collective-permute-done((bf16[8,16,1024]{2,1,0:T(8,128)(2,1)S(1)}, bf16[8,16,1024]{2,1,0:T(8,128)(2,1)S(1)}, u32[]{:S(2)}, u32[]{:S(2)}) %collective-permute-start.7) | collective-permute-done | bytes 262176 | tf_op jit(solution)/shard_map/ppermute | solution.py:211
  118.1 0.0 collective-permute-done.10.refs_12_
  118.1 0.0 copy-done
  118.1 0.0 copy-done.1
  118.1 4.7 %ladder.1 = (f32[2,4,32,512]{3,2,1,0:T(8,128)S(1)}, f32[2,4,32,512]{3,2,1,0:T(8,128)S(1)}) custom-call(s32[4]{0:T(128)S(1)} %copy-done.1, bf16[16,16,1024]{2,1,0:T(8,128)(2,1)S(1)} %all_to_all.10.refs_0_, bf16[16,16,1024]{2,1,0:T(8,128)(2,1)S(1)} %collective-permute-done.refs_1_, bf16[16,16,1024]{2,1,0:T(8,128)(2,1)S(1)} %collective-permute-done.1.refs_2_, ...), custom_call_target="tpu_custom_call" | custom-call | flops 2147483648 | bytes 10485760 | tf_op jit(solution)/shard_map/ladder/pallas_call | solution.py:215
  122.8 1.9 %collective-permute-start.11 = (f32[2,4,32,512]{3,2,1,0:T(8,128)S(1)}, f32[2,4,32,512]{3,2,1,0:T(8,128)S(1)}, u32[]{:S(2)}, u32[]{:S(2)}) collective-permute-start(f32[2,4,32,512]{3,2,1,0:T(8,128)S(1)} %get-tuple-element.14), channel_id=1, source_target_pairs={{0,1},{1,0},{2,3},{3,2},{4,5},{5,4},{6,7},{7,6},{8,9},{9,8},{10,11... | collective-permute-start | bytes 1572872 | tf_op jit(solution)/shard_map/ppermute | solution.py:231
  124.7 1.9 %collective-permute-done.11 = f32[2,4,32,512]{3,2,1,0:T(8,128)S(1)} collective-permute-done((f32[2,4,32,512]{3,2,1,0:T(8,128)S(1)}, f32[2,4,32,512]{3,2,1,0:T(8,128)S(1)}, u32[]{:S(2)}, u32[]{:S(2)}) %collective-permute-start.11) | collective-permute-done | bytes 524320 | tf_op jit(solution)/shard_map/ppermute | solution.py:231
  126.6 0.1 add.19
  126.7 2.1 %collective-permute-start.12 = (f32[4,32,512]{2,1,0:T(8,128)S(1)}, f32[4,32,512]{2,1,0:T(8,128)S(1)}, u32[]{:S(2)}, u32[]{:S(2)}) collective-permute-start(f32[4,32,512]{2,1,0:T(8,128)S(1)} %slice_bitcast_fusion.1), channel_id=1, source_target_pairs={{0,2},{2,0},{1,3},{3,1},{4,6},{6,4},{5,7},{7,5},{8,10},{10,8},{9,1... | collective-permute-start | bytes 786440 | tf_op jit(solution)/shard_map/ppermute | solution.py:232
  128.8 8.1 %collective-permute-done.12 = f32[4,32,512]{2,1,0:T(8,128)S(1)} collective-permute-done((f32[4,32,512]{2,1,0:T(8,128)S(1)}, f32[4,32,512]{2,1,0:T(8,128)S(1)}, u32[]{:S(2)}, u32[]{:S(2)}) %collective-permute-start.12) | collective-permute-done | bytes 262176 | tf_op jit(solution)/shard_map/ppermute | solution.py:232
  137.0 17.4 %all_to_all.11 = bf16[4,32,512]{2,1,0:T(8,128)(2,1)S(1)} all-to-all(bf16[4,32,512]{2,1,0:T(8,128)(2,1)S(1)} %fusion.1), channel_id=1, replica_groups=mesh['ylo'=4,'z'=8,'yhi'=2,'xh'=2,'xp'=2,'core'=2] {'yhi','xh'}, dimensions={0} | all-to-all | bytes 262144 | tf_op jit(solution)/shard_map/all_to_all | solution.py:233
  154.4 0.7 copy.6
  (4 shorter events, 0.1 us)
Async XLA Ops:
  7.1 81.2 %collective-permute-start.9 = (bf16[2,4,128,1024]{3,2,1,0:T(8,128)(2,1)}, bf16[2,4,128,1024]{3,2,1,0:T(8,128)(2,1)S(1)}, u32[]{:S(2)}, u32[]{:S(2)}) collective-permute-start(bf16[2,4,128,1024]{3,2,1,0:T(8,128)(2,1)} %get-tuple-element.12), channel_id=1, source_target_pairs={{0,2},{2,0},{1,3},{3,1},{4,6},{6,4},{5,7},{7,5},{8,10},{10,8},{9,1... | collective-permute-start | bytes 6291464 | tf_op jit(solution)/shard_map/ppermute | solution.py:201
  13.0 105.1 %copy-start = (bf16[4,128,1024]{2,1,0:T(8,128)(2,1)S(1)}, bf16[4,128,1024]{2,1,0:T(8,128)(2,1)}, u32[]{:S(2)}) copy-start(bf16[4,128,1024]{2,1,0:T(8,128)(2,1)} %get-tuple-element.10.refs_9_) | copy-start | bytes 3145732
  13.0 105.1 %copy-start.1 = (s32[4]{0:T(128)S(1)}, s32[4]{0:T(128)}, u32[]{:S(2)}) copy-start(s32[4]{0:T(128)} %pad_add_fusion.meta) | copy-start | bytes 52
  64.4 15.3 %collective-permute-start.1 = (bf16[16,16,1024]{2,1,0:T(8,128)(2,1)S(1)}, bf16[16,16,1024]{2,1,0:T(8,128)(2,1)S(1)}, u32[]{:S(2)}, u32[]{:S(2)}) collective-permute-start(bf16[16,16,1024]{2,1,0:T(8,128)(2,1)S(1)} %all_to_all.10.refs_0_), channel_id=1, source_target_pairs={{0,16},{1,129},{2,18},{3,131},{4,20},{5,133},{6,22},{7,135},{8,24}... | collective-permute-start | bytes 1572872 | tf_op jit(solution)/shard_map/ppermute | solution.py:208
  68.7 17.7 %collective-permute-start = (bf16[16,16,1024]{2,1,0:T(8,128)(2,1)S(1)}, bf16[16,16,1024]{2,1,0:T(8,128)(2,1)S(1)}, u32[]{:S(2)}, u32[]{:S(2)}) collective-permute-start(bf16[16,16,1024]{2,1,0:T(8,128)(2,1)S(1)} %all_to_all.10.refs_0_), channel_id=1, source_target_pairs={{0,112},{1,393},{2,114},{3,395},{4,116},{5,397},{6,118},{7,399},{8... | collective-permute-start | bytes 1572872 | tf_op jit(solution)/shard_map/ppermute | solution.py:209
  77.8 33.9 %collective-permute-start.8 = (bf16[4,128,1024]{2,1,0:T(8,128)(2,1)}, bf16[4,128,1024]{2,1,0:T(8,128)(2,1)S(1)}, u32[]{:S(2)}, u32[]{:S(2)}) collective-permute-start(bf16[4,128,1024]{2,1,0:T(8,128)(2,1)} %get-tuple-element.11), channel_id=1, source_target_pairs={{0,1},{1,0},{2,3},{3,2},{4,5},{5,4},{6,7},{7,6},{8,9},{9,8},{10,11... | collective-permute-start | bytes 3145736 | tf_op jit(solution)/shard_map/ppermute | solution.py:202
  79.8 13.8 %collective-permute-start.2 = (bf16[16,16,1024]{2,1,0:T(8,128)(2,1)S(1)}, bf16[16,16,1024]{2,1,0:T(8,128)(2,1)S(1)}, u32[]{:S(2)}, u32[]{:S(2)}) collective-permute-start(bf16[16,16,1024]{2,1,0:T(8,128)(2,1)S(1)} %collective-permute-done.1.refs_2_), channel_id=1, source_target_pairs={{0,112},{1,393},{2,114},{3,395},{4,116},{5,397},{6,118},{7,399},{8... | collective-permute-start | bytes 1572872 | tf_op jit(solution)/shard_map/ppermute | solution.py:209
  86.4 11.1 %collective-permute-start.3 = (bf16[16,16,1024]{2,1,0:T(8,128)(2,1)S(1)}, bf16[16,16,1024]{2,1,0:T(8,128)(2,1)S(1)}, u32[]{:S(2)}, u32[]{:S(2)}) collective-permute-start(bf16[16,16,1024]{2,1,0:T(8,128)(2,1)S(1)} %collective-permute-done.refs_1_), channel_id=1, source_target_pairs={{0,16},{1,129},{2,18},{3,131},{4,20},{5,133},{6,22},{7,135},{8,24}... | collective-permute-start | bytes 1572872 | tf_op jit(solution)/shard_map/ppermute | solution.py:208
  88.4 29.6 %collective-permute-start.10 = (bf16[4,128,1024]{2,1,0:T(8,128)(2,1)S(1)}, bf16[4,128,1024]{2,1,0:T(8,128)(2,1)S(1)}, u32[]{:S(2)}, u32[]{:S(2)}) collective-permute-start(bf16[4,128,1024]{2,1,0:T(8,128)(2,1)S(1)} %slice_bitcast_fusion), channel_id=1, source_target_pairs={{0,1},{1,0},{2,3},{3,2},{4,5},{5,4},{6,7},{7,6},{8,9},{9,8},{10,11... | collective-permute-start | bytes 3145736 | tf_op jit(solution)/shard_map/ppermute | solution.py:203
  93.6 11.1 %collective-permute-start.5 = (bf16[16,16,1024]{2,1,0:T(8,128)(2,1)S(1)}, bf16[16,16,1024]{2,1,0:T(8,128)(2,1)S(1)}, u32[]{:S(2)}, u32[]{:S(2)}) collective-permute-start(bf16[16,16,1024]{2,1,0:T(8,128)(2,1)S(1)} %collective-permute-done.2.refs_3_), channel_id=1, source_target_pairs={{0,16},{1,129},{2,18},{3,131},{4,20},{5,133},{6,22},{7,135},{8,24}... | collective-permute-start | bytes 1572872 | tf_op jit(solution)/shard_map/ppermute | solution.py:208
  97.5 12.3 %collective-permute-start.4 = (bf16[16,16,1024]{2,1,0:T(8,128)(2,1)S(1)}, bf16[16,16,1024]{2,1,0:T(8,128)(2,1)S(1)}, u32[]{:S(2)}, u32[]{:S(2)}) collective-permute-start(bf16[16,16,1024]{2,1,0:T(8,128)(2,1)S(1)} %collective-permute-done.3.refs_4_), channel_id=1, source_target_pairs={{0,112},{1,393},{2,114},{3,395},{4,116},{5,397},{6,118},{7,399},{8... | collective-permute-start | bytes 1572872 | tf_op jit(solution)/shard_map/ppermute | solution.py:209
  104.7 9.5 %collective-permute-start.6 = (bf16[8,16,1024]{2,1,0:T(8,128)(2,1)S(1)}, bf16[8,16,1024]{2,1,0:T(8,128)(2,1)S(1)}, u32[]{:S(2)}, u32[]{:S(2)}) collective-permute-start(bf16[8,16,1024]{2,1,0:T(8,128)(2,1)S(1)} %slice.20), channel_id=1, source_target_pairs={{0,112},{1,393},{2,114},{3,395},{4,116},{5,397},{6,118},{7,399},{8... | collective-permute-start | bytes 786440 | tf_op jit(solution)/shard_map/ppermute | solution.py:210
  109.8 8.3 %collective-permute-start.7 = (bf16[8,16,1024]{2,1,0:T(8,128)(2,1)S(1)}, bf16[8,16,1024]{2,1,0:T(8,128)(2,1)S(1)}, u32[]{:S(2)}, u32[]{:S(2)}) collective-permute-start(bf16[8,16,1024]{2,1,0:T(8,128)(2,1)S(1)} %slice.21), channel_id=1, source_target_pairs={{0,16},{1,129},{2,18},{3,131},{4,20},{5,133},{6,22},{7,135},{8,24}... | collective-permute-start | bytes 786440 | tf_op jit(solution)/shard_map/ppermute | solution.py:211
  122.8 3.8 %collective-permute-start.11 = (f32[2,4,32,512]{3,2,1,0:T(8,128)S(1)}, f32[2,4,32,512]{3,2,1,0:T(8,128)S(1)}, u32[]{:S(2)}, u32[]{:S(2)}) collective-permute-start(f32[2,4,32,512]{3,2,1,0:T(8,128)S(1)} %get-tuple-element.14), channel_id=1, source_target_pairs={{0,1},{1,0},{2,3},{3,2},{4,5},{5,4},{6,7},{7,6},{8,9},{9,8},{10,11... | collective-permute-start | bytes 1572872 | tf_op jit(solution)/shard_map/ppermute | solution.py:231
  126.7 10.2 %collective-permute-start.12 = (f32[4,32,512]{2,1,0:T(8,128)S(1)}, f32[4,32,512]{2,1,0:T(8,128)S(1)}, u32[]{:S(2)}, u32[]{:S(2)}) collective-permute-start(f32[4,32,512]{2,1,0:T(8,128)S(1)} %slice_bitcast_fusion.1), channel_id=1, source_target_pairs={{0,2},{2,0},{1,3},{3,1},{4,6},{6,4},{5,7},{7,5},{8,10},{10,8},{9,1... | collective-permute-start | bytes 786440 | tf_op jit(solution)/shard_map/ppermute | solution.py:232

commit v3 on v2

--- a/solution.py
+++ b/solution.py
@@ -139,26 +139,31 @@
                     found.append((source.at[pl.ds(at, Z)], ints.at[(there // YLO) * XH + xh, lax.rem(there, YLO)]))
         return [pltpu.make_async_copy(a, b, sem.at[0]) for a, b in found]
 
-    mine = []
-    for n in range(TEAM):
-        rows = pl.ds(pl.multiple_of((me ^ n) * PAIRS, PAIRS), PAIRS)
-        source = team[n].at[0] if n == 2 else team[n]
-        mine.append(pltpu.make_async_copy(source, amps.at[:, rows], sem.at[0]))
-    for copy in mine:
+    team_loads = []
+    for quad in range(QUADS):
+        for n in range(TEAM):
+            rows = pl.ds(pl.multiple_of((me ^ n) * PAIRS, PAIRS), PAIRS)
+            source = team[n].at[0, quad] if n == 2 else team[n].at[quad]
+            team_loads.append(pltpu.make_async_copy(source, amps.at[quad, rows], sem.at[1 + quad]))
+    for on in range(CORE):
+
+        @pl.when(core == on)
+        def _():
+            for copy in copies(on):
+                copy.start()
+
+    for copy in team_loads:
         copy.start()
     for on in range(CORE):
 
         @pl.when(core == on)
         def _():
-            todo = copies(on)
-            for copy in todo:
-                copy.start()
-            for copy in todo:
+            for copy in copies(on):
                 copy.wait()
 
-    for copy in mine:
-        copy.wait()
     for panel in range(QUADS):
+        for copy in team_loads[panel * TEAM : (panel + 1) * TEAM]:
+            copy.wait()
         product = lax.dot_general(
             ints[panel].reshape(YLO * Z * ROWS, PANEL),
             amps[panel],
@@ -222,7 +227,7 @@
             pltpu.VMEM((QUADS, YLO, Z, ROWS, PANEL), jnp.bfloat16),
             pltpu.VMEM((QUADS, TEAM * PAIRS, PANEL), jnp.bfloat16),
             pltpu.VMEM((QUADS, TEAM, 32, TEAM * PAIRS), jnp.float32),
-            pltpu.SemaphoreType.DMA((1,)),
+            pltpu.SemaphoreType.DMA((1 + QUADS,)),
         ],
         compiler_params=pltpu.CompilerParams(vmem_limit_bytes=24 << 20),
         cost_estimate=pl.CostEstimate(flops=2 << 30, bytes_accessed=10 << 20, transcendentals=0),

time: 156 us -> 156 us (level)
  no operation moved by 1% of the time
where the time goes in v3:
time: 156 us; the launch traced here: 155 us
  blocking collectives  68.8 us (44%)
  starting transfers between devices  45.9 us (29%)
  waiting for transfers between devices  25 us (16%)
  Pallas kernels  13.9 us (9%)
    all_to_all x1, blocking collectives, compute(): lax.all_to_all(panels, ALL, 0, 0, axis_index_groups=plane_groups(), tiled...  51.4 us
    ppermute x3, starting transfers between devices, compute(): have[-step] = lax.ppermute(have[step - 1], ALL, odd)  19.4 us
    all_to_all x1, blocking collectives, compute(): pieces = lax.all_to_all(summed, ('yhi', 'xh'), 0, 0, tiled=True)  17.4 us
    ppermute x1, waiting for transfers between devices, compute(): lax.ppermute(pair[1], 'xp', [(0, 1), (1, 0)])  8.11 us
    ppermute x3, starting transfers between devices, compute(): have[step] = lax.ppermute(have[1 - step], ALL, even)  8.1 us
    pallas_call x1, Pallas kernels, split_amplitudes(): pl.pallas_call(split_kernel, in_specs=[pl.BlockSpec(memory_space=pltpu.SM...  6.47 us
    ppermute x3, waiting for transfers between devices, compute(): have[step] = lax.ppermute(have[1 - step], ALL, even)  5.49 us
    ppermute x1, starting transfers between devices, compute(): last_odd = lax.ppermute(have[3][:8], ALL, odd)  5.13 us
  transfers between devices with their start and end apart: 13, of which 7 were waited for; matrix products, arithmetic and copies ran while one was open for 0% of the time, Pallas kernels for 2%

profile of v3, /device:TPU:8, one launch (start us, length us, event | category | flops | bytes accessed | tf_op | source)
XLA Modules:
  0.0 155.4 jit_solution(12661356364895082898)
XLA Ops:
  0.0 0.6 pad_add_fusion.meta
  0.6 6.5 %split_amplitudes.1 = (bf16[4,128,1024]{2,1,0:T(8,128)(2,1)}, bf16[4,128,1024]{2,1,0:T(8,128)(2,1)}, bf16[2,4,128,1024]{3,2,1,0:T(8,128)(2,1)}) custom-call(s32[4]{0:T(128)} %pad_add_fusion.meta, bf16[128,16384]{1,0:T(8,128)(2,1)} %amps.1, s32[2,256]{1,0:T(2,128)} %tiles.1), custom_call_target="tpu_custom_call" | custom-call | flops 8388608 | bytes 8388608 | tf_op jit(solution)/shard_map/split_amplitudes/pallas_call | solution.py:101
  7.1 3.4 %collective-permute-start.9 = (bf16[2,4,128,1024]{3,2,1,0:T(8,128)(2,1)}, bf16[2,4,128,1024]{3,2,1,0:T(8,128)(2,1)S(1)}, u32[]{:S(2)}, u32[]{:S(2)}) collective-permute-start(bf16[2,4,128,1024]{3,2,1,0:T(8,128)(2,1)} %get-tuple-element.12), channel_id=1, source_target_pairs={{0,2},{2,0},{1,3},{3,1},{4,6},{6,4},{5,7},{7,5},{8,10},{10,8},{9,1... | collective-permute-start | bytes 6291464 | tf_op jit(solution)/shard_map/ppermute | solution.py:206
  10.5 2.4 %mask_integrals.1 = bf16[16,16,1024]{2,1,0:T(8,128)(2,1)} custom-call(s32[4]{0:T(128)} %pad_add_fusion.meta, bf16[16,1024]{1,0:T(8,128)(2,1)} %ints_hbm.1, s32[8,16]{1,0:T(8,128)} %tiles_hbm.1), custom_call_target="tpu_custom_call" | custom-call | tf_op jit(solution)/shard_map/mask_integrals/pallas_call | solution.py:190
  13.0 0.0 copy-start
  13.0 0.0 copy-start.1
  13.0 51.4 %all_to_all.10.refs_0_ = bf16[16,16,1024]{2,1,0:T(8,128)(2,1)S(1)} all-to-all(bf16[16,16,1024]{2,1,0:T(8,128)(2,1)} %mask_integrals.1), channel_id=1, replica_groups={{0,128,256,384,8,136,264,392,4,132,260,388,12,140,268,396},{16,144,272,..., dimensions={0} | all-to-all | bytes 1048576 | tf_op jit(solution)/shard_map/all_to_all | solution.py:203
  64.4 4.3 %collective-permute-start.1 = (bf16[16,16,1024]{2,1,0:T(8,128)(2,1)S(1)}, bf16[16,16,1024]{2,1,0:T(8,128)(2,1)S(1)}, u32[]{:S(2)}, u32[]{:S(2)}) collective-permute-start(bf16[16,16,1024]{2,1,0:T(8,128)(2,1)S(1)} %all_to_all.10.refs_0_), channel_id=1, source_target_pairs={{0,16},{1,129},{2,18},{3,131},{4,20},{5,133},{6,22},{7,135},{8,24}... | collective-permute-start | bytes 1572872 | tf_op jit(solution)/shard_map/ppermute | solution.py:213
  68.7 9.1 %collective-permute-start = (bf16[16,16,1024]{2,1,0:T(8,128)(2,1)S(1)}, bf16[16,16,1024]{2,1,0:T(8,128)(2,1)S(1)}, u32[]{:S(2)}, u32[]{:S(2)}) collective-permute-start(bf16[16,16,1024]{2,1,0:T(8,128)(2,1)S(1)} %all_to_all.10.refs_0_), channel_id=1, source_target_pairs={{0,112},{1,393},{2,114},{3,395},{4,116},{5,397},{6,118},{7,399},{8... | collective-permute-start | bytes 1572872 | tf_op jit(solution)/shard_map/ppermute | solution.py:214
  77.8 1.9 %collective-permute-start.8 = (bf16[4,128,1024]{2,1,0:T(8,128)(2,1)}, bf16[4,128,1024]{2,1,0:T(8,128)(2,1)S(1)}, u32[]{:S(2)}, u32[]{:S(2)}) collective-permute-start(bf16[4,128,1024]{2,1,0:T(8,128)(2,1)} %get-tuple-element.11), channel_id=1, source_target_pairs={{0,1},{1,0},{2,3},{3,2},{4,5},{5,4},{6,7},{7,6},{8,9},{9,8},{10,11... | collective-permute-start | bytes 3145736 | tf_op jit(solution)/shard_map/ppermute | solution.py:207
  79.8 0.0 collective-permute-done.1.refs_2_
  79.8 6.6 %collective-permute-start.2 = (bf16[16,16,1024]{2,1,0:T(8,128)(2,1)S(1)}, bf16[16,16,1024]{2,1,0:T(8,128)(2,1)S(1)}, u32[]{:S(2)}, u32[]{:S(2)}) collective-permute-start(bf16[16,16,1024]{2,1,0:T(8,128)(2,1)S(1)} %collective-permute-done.1.refs_2_), channel_id=1, source_target_pairs={{0,112},{1,393},{2,114},{3,395},{4,116},{5,397},{6,118},{7,399},{8... | collective-permute-start | bytes 1572872 | tf_op jit(solution)/shard_map/ppermute | solution.py:214
  86.4 0.0 collective-permute-done.refs_1_
  86.4 1.9 %collective-permute-start.3 = (bf16[16,16,1024]{2,1,0:T(8,128)(2,1)S(1)}, bf16[16,16,1024]{2,1,0:T(8,128)(2,1)S(1)}, u32[]{:S(2)}, u32[]{:S(2)}) collective-permute-start(bf16[16,16,1024]{2,1,0:T(8,128)(2,1)S(1)} %collective-permute-done.refs_1_), channel_id=1, source_target_pairs={{0,16},{1,129},{2,18},{3,131},{4,20},{5,133},{6,22},{7,135},{8,24}... | collective-permute-start | bytes 1572872 | tf_op jit(solution)/shard_map/ppermute | solution.py:213
  88.4 0.0 collective-permute-done.9.refs_11_
  88.4 0.1 slice_bitcast_fusion
  88.4 1.9 %collective-permute-start.10 = (bf16[4,128,1024]{2,1,0:T(8,128)(2,1)S(1)}, bf16[4,128,1024]{2,1,0:T(8,128)(2,1)S(1)}, u32[]{:S(2)}, u32[]{:S(2)}) collective-permute-start(bf16[4,128,1024]{2,1,0:T(8,128)(2,1)S(1)} %slice_bitcast_fusion), channel_id=1, source_target_pairs={{0,1},{1,0},{2,3},{3,2},{4,5},{5,4},{6,7},{7,6},{8,9},{9,8},{10,11... | collective-permute-start | bytes 3145736 | tf_op jit(solution)/shard_map/ppermute | solution.py:208
  90.4 3.2 %collective-permute-done.2.refs_3_ = bf16[16,16,1024]{2,1,0:T(8,128)(2,1)S(1)} collective-permute-done((bf16[16,16,1024]{2,1,0:T(8,128)(2,1)S(1)}, bf16[16,16,1024]{2,1,0:T(8,128)(2,1)S(1)}, u32[]{:S(2)}, u32[]{:S(2)}) %collective-permute-start.2) | collective-permute-done | bytes 524320 | tf_op jit(solution)/shard_map/ppermute | solution.py:214
  93.6 1.9 %collective-permute-start.5 = (bf16[16,16,1024]{2,1,0:T(8,128)(2,1)S(1)}, bf16[16,16,1024]{2,1,0:T(8,128)(2,1)S(1)}, u32[]{:S(2)}, u32[]{:S(2)}) collective-permute-start(bf16[16,16,1024]{2,1,0:T(8,128)(2,1)S(1)} %collective-permute-done.2.refs_3_), channel_id=1, source_target_pairs={{0,16},{1,129},{2,18},{3,131},{4,20},{5,133},{6,22},{7,135},{8,24}... | collective-permute-start | bytes 1572872 | tf_op jit(solution)/shard_map/ppermute | solution.py:213
  95.5 2.0 %collective-permute-done.3.refs_4_ = bf16[16,16,1024]{2,1,0:T(8,128)(2,1)S(1)} collective-permute-done((bf16[16,16,1024]{2,1,0:T(8,128)(2,1)S(1)}, bf16[16,16,1024]{2,1,0:T(8,128)(2,1)S(1)}, u32[]{:S(2)}, u32[]{:S(2)}) %collective-permute-start.3) | collective-permute-done | bytes 524320 | tf_op jit(solution)/shard_map/ppermute | solution.py:213
  97.5 3.6 %collective-permute-start.4 = (bf16[16,16,1024]{2,1,0:T(8,128)(2,1)S(1)}, bf16[16,16,1024]{2,1,0:T(8,128)(2,1)S(1)}, u32[]{:S(2)}, u32[]{:S(2)}) collective-permute-start(bf16[16,16,1024]{2,1,0:T(8,128)(2,1)S(1)} %collective-permute-done.3.refs_4_), channel_id=1, source_target_pairs={{0,112},{1,393},{2,114},{3,395},{4,116},{5,397},{6,118},{7,399},{8... | collective-permute-start | bytes 1572872 | tf_op jit(solution)/shard_map/ppermute | solution.py:214
  101.2 3.5 %collective-permute-done.5.refs_6_ = bf16[16,16,1024]{2,1,0:T(8,128)(2,1)S(1)} collective-permute-done((bf16[16,16,1024]{2,1,0:T(8,128)(2,1)S(1)}, bf16[16,16,1024]{2,1,0:T(8,128)(2,1)S(1)}, u32[]{:S(2)}, u32[]{:S(2)}) %collective-permute-start.5) | collective-permute-done | bytes 524320 | tf_op jit(solution)/shard_map/ppermute | solution.py:213
  104.7 5.1 %collective-permute-start.6 = (bf16[8,16,1024]{2,1,0:T(8,128)(2,1)S(1)}, bf16[8,16,1024]{2,1,0:T(8,128)(2,1)S(1)}, u32[]{:S(2)}, u32[]{:S(2)}) collective-permute-start(bf16[8,16,1024]{2,1,0:T(8,128)(2,1)S(1)} %slice.20), channel_id=1, source_target_pairs={{0,112},{1,393},{2,114},{3,395},{4,116},{5,397},{6,118},{7,399},{8... | collective-permute-start | bytes 786440 | tf_op jit(solution)/shard_map/ppermute | solution.py:215
  109.8 0.0 collective-permute-done.4.refs_5_
  109.8 1.9 %collective-permute-start.7 = (bf16[8,16,1024]{2,1,0:T(8,128)(2,1)S(1)}, bf16[8,16,1024]{2,1,0:T(8,128)(2,1)S(1)}, u32[]{:S(2)}, u32[]{:S(2)}) collective-permute-start(bf16[8,16,1024]{2,1,0:T(8,128)(2,1)S(1)} %slice.21), channel_id=1, source_target_pairs={{0,16},{1,129},{2,18},{3,131},{4,20},{5,133},{6,22},{7,135},{8,24}... | collective-permute-start | bytes 786440 | tf_op jit(solution)/shard_map/ppermute | solution.py:216
  111.8 0.0 collective-permute-done.8.refs_10_
  111.8 2.4 %collective-permute-done.6.refs_7_ = bf16[8,16,1024]{2,1,0:T(8,128)(2,1)S(1)} collective-permute-done((bf16[8,16,1024]{2,1,0:T(8,128)(2,1)S(1)}, bf16[8,16,1024]{2,1,0:T(8,128)(2,1)S(1)}, u32[]{:S(2)}, u32[]{:S(2)}) %collective-permute-start.6) | collective-permute-done | bytes 262176 | tf_op jit(solution)/shard_map/ppermute | solution.py:215
  114.1 4.0 %collective-permute-done.7.refs_8_ = bf16[8,16,1024]{2,1,0:T(8,128)(2,1)S(1)} collective-permute-done((bf16[8,16,1024]{2,1,0:T(8,128)(2,1)S(1)}, bf16[8,16,1024]{2,1,0:T(8,128)(2,1)S(1)}, u32[]{:S(2)}, u32[]{:S(2)}) %collective-permute-start.7) | collective-permute-done | bytes 262176 | tf_op jit(solution)/shard_map/ppermute | solution.py:216
  118.1 0.0 collective-permute-done.10.refs_12_
  118.1 0.0 copy-done
  118.1 0.0 copy-done.1
  118.1 5.0 %ladder.1 = (f32[2,4,32,512]{3,2,1,0:T(8,128)S(1)}, f32[2,4,32,512]{3,2,1,0:T(8,128)S(1)}) custom-call(s32[4]{0:T(128)S(1)} %copy-done.1, bf16[16,16,1024]{2,1,0:T(8,128)(2,1)S(1)} %all_to_all.10.refs_0_, bf16[16,16,1024]{2,1,0:T(8,128)(2,1)S(1)} %collective-permute-done.refs_1_, bf16[16,16,1024]{2,1,0:T(8,128)(2,1)S(1)} %collective-permute-done.1.refs_2_, ...), custom_call_target="tpu_custom_call" | custom-call | flops 2147483648 | bytes 10485760 | tf_op jit(solution)/shard_map/ladder/pallas_call | solution.py:220
  123.2 1.9 %collective-permute-start.11 = (f32[2,4,32,512]{3,2,1,0:T(8,128)S(1)}, f32[2,4,32,512]{3,2,1,0:T(8,128)S(1)}, u32[]{:S(2)}, u32[]{:S(2)}) collective-permute-start(f32[2,4,32,512]{3,2,1,0:T(8,128)S(1)} %get-tuple-element.14), channel_id=1, source_target_pairs={{0,1},{1,0},{2,3},{3,2},{4,5},{5,4},{6,7},{7,6},{8,9},{9,8},{10,11... | collective-permute-start | bytes 1572872 | tf_op jit(solution)/shard_map/ppermute | solution.py:236
  125.1 1.9 %collective-permute-done.11 = f32[2,4,32,512]{3,2,1,0:T(8,128)S(1)} collective-permute-done((f32[2,4,32,512]{3,2,1,0:T(8,128)S(1)}, f32[2,4,32,512]{3,2,1,0:T(8,128)S(1)}, u32[]{:S(2)}, u32[]{:S(2)}) %collective-permute-start.11) | collective-permute-done | bytes 524320 | tf_op jit(solution)/shard_map/ppermute | solution.py:236
  127.0 0.1 add.19
  127.1 2.1 %collective-permute-start.12 = (f32[4,32,512]{2,1,0:T(8,128)S(1)}, f32[4,32,512]{2,1,0:T(8,128)S(1)}, u32[]{:S(2)}, u32[]{:S(2)}) collective-permute-start(f32[4,32,512]{2,1,0:T(8,128)S(1)} %slice_bitcast_fusion.1), channel_id=1, source_target_pairs={{0,2},{2,0},{1,3},{3,1},{4,6},{6,4},{5,7},{7,5},{8,10},{10,8},{9,1... | collective-permute-start | bytes 786440 | tf_op jit(solution)/shard_map/ppermute | solution.py:237
  129.2 8.1 %collective-permute-done.12 = f32[4,32,512]{2,1,0:T(8,128)S(1)} collective-permute-done((f32[4,32,512]{2,1,0:T(8,128)S(1)}, f32[4,32,512]{2,1,0:T(8,128)S(1)}, u32[]{:S(2)}, u32[]{:S(2)}) %collective-permute-start.12) | collective-permute-done | bytes 262176 | tf_op jit(solution)/shard_map/ppermute | solution.py:237
  137.3 17.4 %all_to_all.11 = bf16[4,32,512]{2,1,0:T(8,128)(2,1)S(1)} all-to-all(bf16[4,32,512]{2,1,0:T(8,128)(2,1)S(1)} %fusion.1), channel_id=1, replica_groups=mesh['ylo'=4,'z'=8,'yhi'=2,'xh'=2,'xp'=2,'core'=2] {'yhi','xh'}, dimensions={0} | all-to-all | bytes 262144 | tf_op jit(solution)/shard_map/all_to_all | solution.py:238
  154.7 0.7 copy.6
  (4 shorter events, 0.1 us)
Async XLA Ops:
  7.1 81.2 %collective-permute-start.9 = (bf16[2,4,128,1024]{3,2,1,0:T(8,128)(2,1)}, bf16[2,4,128,1024]{3,2,1,0:T(8,128)(2,1)S(1)}, u32[]{:S(2)}, u32[]{:S(2)}) collective-permute-start(bf16[2,4,128,1024]{3,2,1,0:T(8,128)(2,1)} %get-tuple-element.12), channel_id=1, source_target_pairs={{0,2},{2,0},{1,3},{3,1},{4,6},{6,4},{5,7},{7,5},{8,10},{10,8},{9,1... | collective-permute-start | bytes 6291464 | tf_op jit(solution)/shard_map/ppermute | solution.py:206
  13.0 105.1 %copy-start = (bf16[4,128,1024]{2,1,0:T(8,128)(2,1)S(1)}, bf16[4,128,1024]{2,1,0:T(8,128)(2,1)}, u32[]{:S(2)}) copy-start(bf16[4,128,1024]{2,1,0:T(8,128)(2,1)} %get-tuple-element.10.refs_9_) | copy-start | bytes 3145732
  13.0 105.1 %copy-start.1 = (s32[4]{0:T(128)S(1)}, s32[4]{0:T(128)}, u32[]{:S(2)}) copy-start(s32[4]{0:T(128)} %pad_add_fusion.meta) | copy-start | bytes 52
  64.4 15.3 %collective-permute-start.1 = (bf16[16,16,1024]{2,1,0:T(8,128)(2,1)S(1)}, bf16[16,16,1024]{2,1,0:T(8,128)(2,1)S(1)}, u32[]{:S(2)}, u32[]{:S(2)}) collective-permute-start(bf16[16,16,1024]{2,1,0:T(8,128)(2,1)S(1)} %all_to_all.10.refs_0_), channel_id=1, source_target_pairs={{0,16},{1,129},{2,18},{3,131},{4,20},{5,133},{6,22},{7,135},{8,24}... | collective-permute-start | bytes 1572872 | tf_op jit(solution)/shard_map/ppermute | solution.py:213
  68.7 17.7 %collective-permute-start = (bf16[16,16,1024]{2,1,0:T(8,128)(2,1)S(1)}, bf16[16,16,1024]{2,1,0:T(8,128)(2,1)S(1)}, u32[]{:S(2)}, u32[]{:S(2)}) collective-permute-start(bf16[16,16,1024]{2,1,0:T(8,128)(2,1)S(1)} %all_to_all.10.refs_0_), channel_id=1, source_target_pairs={{0,112},{1,393},{2,114},{3,395},{4,116},{5,397},{6,118},{7,399},{8... | collective-permute-start | bytes 1572872 | tf_op jit(solution)/shard_map/ppermute | solution.py:214
  77.8 33.9 %collective-permute-start.8 = (bf16[4,128,1024]{2,1,0:T(8,128)(2,1)}, bf16[4,128,1024]{2,1,0:T(8,128)(2,1)S(1)}, u32[]{:S(2)}, u32[]{:S(2)}) collective-permute-start(bf16[4,128,1024]{2,1,0:T(8,128)(2,1)} %get-tuple-element.11), channel_id=1, source_target_pairs={{0,1},{1,0},{2,3},{3,2},{4,5},{5,4},{6,7},{7,6},{8,9},{9,8},{10,11... | collective-permute-start | bytes 3145736 | tf_op jit(solution)/shard_map/ppermute | solution.py:207
  79.8 13.8 %collective-permute-start.2 = (bf16[16,16,1024]{2,1,0:T(8,128)(2,1)S(1)}, bf16[16,16,1024]{2,1,0:T(8,128)(2,1)S(1)}, u32[]{:S(2)}, u32[]{:S(2)}) collective-permute-start(bf16[16,16,1024]{2,1,0:T(8,128)(2,1)S(1)} %collective-permute-done.1.refs_2_), channel_id=1, source_target_pairs={{0,112},{1,393},{2,114},{3,395},{4,116},{5,397},{6,118},{7,399},{8... | collective-permute-start | bytes 1572872 | tf_op jit(solution)/shard_map/ppermute | solution.py:214
  86.4 11.1 %collective-permute-start.3 = (bf16[16,16,1024]{2,1,0:T(8,128)(2,1)S(1)}, bf16[16,16,1024]{2,1,0:T(8,128)(2,1)S(1)}, u32[]{:S(2)}, u32[]{:S(2)}) collective-permute-start(bf16[16,16,1024]{2,1,0:T(8,128)(2,1)S(1)} %collective-permute-done.refs_1_), channel_id=1, source_target_pairs={{0,16},{1,129},{2,18},{3,131},{4,20},{5,133},{6,22},{7,135},{8,24}... | collective-permute-start | bytes 1572872 | tf_op jit(solution)/shard_map/ppermute | solution.py:213
  88.4 29.6 %collective-permute-start.10 = (bf16[4,128,1024]{2,1,0:T(8,128)(2,1)S(1)}, bf16[4,128,1024]{2,1,0:T(8,128)(2,1)S(1)}, u32[]{:S(2)}, u32[]{:S(2)}) collective-permute-start(bf16[4,128,1024]{2,1,0:T(8,128)(2,1)S(1)} %slice_bitcast_fusion), channel_id=1, source_target_pairs={{0,1},{1,0},{2,3},{3,2},{4,5},{5,4},{6,7},{7,6},{8,9},{9,8},{10,11... | collective-permute-start | bytes 3145736 | tf_op jit(solution)/shard_map/ppermute | solution.py:208
  93.6 11.1 %collective-permute-start.5 = (bf16[16,16,1024]{2,1,0:T(8,128)(2,1)S(1)}, bf16[16,16,1024]{2,1,0:T(8,128)(2,1)S(1)}, u32[]{:S(2)}, u32[]{:S(2)}) collective-permute-start(bf16[16,16,1024]{2,1,0:T(8,128)(2,1)S(1)} %collective-permute-done.2.refs_3_), channel_id=1, source_target_pairs={{0,16},{1,129},{2,18},{3,131},{4,20},{5,133},{6,22},{7,135},{8,24}... | collective-permute-start | bytes 1572872 | tf_op jit(solution)/shard_map/ppermute | solution.py:213
  97.5 12.3 %collective-permute-start.4 = (bf16[16,16,1024]{2,1,0:T(8,128)(2,1)S(1)}, bf16[16,16,1024]{2,1,0:T(8,128)(2,1)S(1)}, u32[]{:S(2)}, u32[]{:S(2)}) collective-permute-start(bf16[16,16,1024]{2,1,0:T(8,128)(2,1)S(1)} %collective-permute-done.3.refs_4_), channel_id=1, source_target_pairs={{0,112},{1,393},{2,114},{3,395},{4,116},{5,397},{6,118},{7,399},{8... | collective-permute-start | bytes 1572872 | tf_op jit(solution)/shard_map/ppermute | solution.py:214
  104.7 9.5 %collective-permute-start.6 = (bf16[8,16,1024]{2,1,0:T(8,128)(2,1)S(1)}, bf16[8,16,1024]{2,1,0:T(8,128)(2,1)S(1)}, u32[]{:S(2)}, u32[]{:S(2)}) collective-permute-start(bf16[8,16,1024]{2,1,0:T(8,128)(2,1)S(1)} %slice.20), channel_id=1, source_target_pairs={{0,112},{1,393},{2,114},{3,395},{4,116},{5,397},{6,118},{7,399},{8... | collective-permute-start | bytes 786440 | tf_op jit(solution)/shard_map/ppermute | solution.py:215
  109.8 8.3 %collective-permute-start.7 = (bf16[8,16,1024]{2,1,0:T(8,128)(2,1)S(1)}, bf16[8,16,1024]{2,1,0:T(8,128)(2,1)S(1)}, u32[]{:S(2)}, u32[]{:S(2)}) collective-permute-start(bf16[8,16,1024]{2,1,0:T(8,128)(2,1)S(1)} %slice.21), channel_id=1, source_target_pairs={{0,16},{1,129},{2,18},{3,131},{4,20},{5,133},{6,22},{7,135},{8,24}... | collective-permute-start | bytes 786440 | tf_op jit(solution)/shard_map/ppermute | solution.py:216
  123.2 3.8 %collective-permute-start.11 = (f32[2,4,32,512]{3,2,1,0:T(8,128)S(1)}, f32[2,4,32,512]{3,2,1,0:T(8,128)S(1)}, u32[]{:S(2)}, u32[]{:S(2)}) collective-permute-start(f32[2,4,32,512]{3,2,1,0:T(8,128)S(1)} %get-tuple-element.14), channel_id=1, source_target_pairs={{0,1},{1,0},{2,3},{3,2},{4,5},{5,4},{6,7},{7,6},{8,9},{9,8},{10,11... | collective-permute-start | bytes 1572872 | tf_op jit(solution)/shard_map/ppermute | solution.py:236
  127.1 10.2 %collective-permute-start.12 = (f32[4,32,512]{2,1,0:T(8,128)S(1)}, f32[4,32,512]{2,1,0:T(8,128)S(1)}, u32[]{:S(2)}, u32[]{:S(2)}) collective-permute-start(f32[4,32,512]{2,1,0:T(8,128)S(1)} %slice_bitcast_fusion.1), channel_id=1, source_target_pairs={{0,2},{2,0},{1,3},{3,1},{4,6},{6,4},{5,7},{7,5},{8,10},{10,8},{9,1... | collective-permute-start | bytes 786440 | tf_op jit(solution)/shard_map/ppermute | solution.py:237
